TPU v7x, 32 devices: a whole 2x2x4 slice. The times are simulated.
32 devices in a mesh: dp: 4 (over x, core), vocab: 8 (over z, y).
Axes of the slice: x: 2, y: 2, z: 4, core: 2. Of those that a mesh axis runs over, the one named last changes fastest.
Arguments:
- token_ids: int32 [32, 512], P(('dp', 'vocab')), may hold values from 0 to 30719, as said below
- lengths: int32 [32], P(('dp', 'vocab')), may hold values from 1 to 512, as said below
- word_table: bfloat16 [30720, 768], P('vocab'), may hold values from -6 to 6
- position_table: bfloat16 [512, 768], P('vocab'), may hold values from -3 to 3
- embed_gain: bfloat16 [768], P('vocab'), may hold values from 0.5 to 1.5
- embed_bias: bfloat16 [768], P('vocab'), may hold values from -3 to 3
- query_weight: bfloat16 [768, 768], P('vocab'), may hold values from -0.21875 to 0.21875
- query_bias: bfloat16 [768], P('vocab'), may hold values from -3 to 3
- key_weight: bfloat16 [768, 768], P('vocab'), may hold values from -0.21875 to 0.21875
- value_weight: bfloat16 [768, 768], P('vocab'), may hold values from -0.21875 to 0.21875
- value_bias: bfloat16 [768], P('vocab'), may hold values from -3 to 3
- output_weight: bfloat16 [768, 768], P('vocab'), may hold values from -0.875 to 0.875
- output_bias: bfloat16 [768], P('vocab'), may hold values from -3 to 3
- middle_gain: bfloat16 [768], P('vocab'), may hold values from 0.5 to 1.5
- middle_bias: bfloat16 [768], P('vocab'), may hold values from -3 to 3
- inner_weight: bfloat16 [768, 3072], P('vocab'), may hold values from -0.21875 to 0.21875
- inner_bias: bfloat16 [3072], P('vocab'), may hold values from -3 to 3
- outer_weight: bfloat16 [3072, 768], P('vocab'), may hold values from -0.109375 to 0.109375
- outer_bias: bfloat16 [768], P('vocab'), may hold values from -3 to 3
- final_gain: bfloat16 [768], P('vocab'), may hold values from 0.5 to 1.5
- final_bias: bfloat16 [768], P('vocab'), may hold values from -3 to 3
- cotangent: bfloat16 [32, 512, 768], P(('dp', 'vocab')), may hold values from -6 to 6
Outputs:
- activations: bfloat16 [32, 512, 768], P(('dp', 'vocab'))
- table_gradient: float32 [30720, 768], P('vocab')
- position_gradient: float32 [512, 768], P('vocab')
- embed_gain_gradient: float32 [768], P('vocab')
- embed_bias_gradient: float32 [768], P('vocab')
- query_weight_gradient: float32 [768, 768], P('vocab')
- query_bias_gradient: float32 [768], P('vocab')
- key_weight_gradient: float32 [768, 768], P('vocab')
- value_weight_gradient: float32 [768, 768], P('vocab')
- value_bias_gradient: float32 [768], P('vocab')
- output_weight_gradient: float32 [768, 768], P('vocab')
- output_bias_gradient: float32 [768], P('vocab')
- middle_gain_gradient: float32 [768], P('vocab')
- middle_bias_gradient: float32 [768], P('vocab')
- inner_weight_gradient: float32 [768, 3072], P('vocab')
- inner_bias_gradient: float32 [3072], P('vocab')
- outer_weight_gradient: float32 [3072, 768], P('vocab')
- outer_bias_gradient: float32 [768], P('vocab')
- final_gain_gradient: float32 [768], P('vocab')
- final_bias_gradient: float32 [768], P('vocab')
Inputs may be any that keep to these rules, and one draw needn't show every extreme that they name: Passage p holds real tokens in its first lengths[p] slots, the rest are padding that no query attends to; some passage is full. `token_ids`: the table's rows fall into equal blocks, one for each index of vocab; of the 512 slots of one device, at most 128 hold ids of one block, and on every device exactly 128 slots hold ids of some block.
All inputs are finite; a program needn't handle non-finite values.
Results may differ from a plain program's by a relative error of at most 0.02.
Values may be sent and summed in bfloat16 or wider, within the bound.
No kernel may reach another device: no remote copies, remote signals or barrier semaphores. Data moves between devices by JAX's collectives and lax.ppermute only.
A program may use at most 192 MiB of HBM per device.

v0:
```python
import math

import jax
import jax.numpy as jnp
from jax import lax
from jax.sharding import PartitionSpec as P

HEADS = 12


epsilon = 1e-12
scaling = 0.125


def normalize(values, gain, bias_row):
    center = values - jnp.mean(values, axis=-1, keepdims=True)
    inverse = lax.rsqrt(jnp.mean(center * center, axis=-1, keepdims=True) + epsilon)
    scaled = center * inverse
    return (scaled * gain + bias_row, scaled, inverse)


def normalize_back(upstream, scaled, inverse, gain):
    weighted = upstream * gain
    return inverse * (
        weighted
        - jnp.mean(weighted, axis=-1, keepdims=True)
        - scaled * jnp.mean(weighted * scaled, axis=-1, keepdims=True)
    )


def gelu_slope(inner):
    cumulative = 0.5 * (1.0 + lax.erf(inner * (1.0 / math.sqrt(2.0))))
    density = jnp.exp(-0.5 * inner * inner) * (1.0 / math.sqrt(2.0 * math.pi))
    return cumulative + inner * density


def matmul(left, right):
    return jnp.dot(left, right, preferred_element_type=jnp.float32)


def contract_rows(left, right):
    return jnp.einsum("ti,tj->ij", left, right, preferred_element_type=jnp.float32)


def times_transposed(left, right):
    return jnp.einsum("tj,ij->ti", left, right, preferred_element_type=jnp.float32)


def split_heads(rows):
    return rows.reshape(rows.shape[0], HEADS, rows.shape[1] // HEADS)


def masked_scores(query_heads, key_heads, visible):
    scores = (
        jnp.einsum("qhd,khd->hqk", query_heads, key_heads, preferred_element_type=jnp.float32)
        * scaling
    )
    return jnp.where(visible[None, None, :], scores, -1e30)


def attend(inputs):
    query_rows, key_rows, value_rows, visible = inputs
    query_heads = split_heads(query_rows)
    scores = masked_scores(query_heads, split_heads(key_rows), visible)
    largest = jnp.max(scores, axis=-1, keepdims=True)
    raised = jnp.exp(scores - largest)
    totals = jnp.sum(raised, axis=-1, keepdims=True)
    probs = raised / totals
    context = jnp.einsum(
        "hqk,khd->qhd",
        probs.astype(jnp.bfloat16),
        split_heads(value_rows),
        preferred_element_type=jnp.float32,
    )
    return (context.reshape(query_rows.shape).astype(jnp.bfloat16), largest + jnp.log(totals))


def attend_back(inputs):
    query_rows, key_rows, value_rows, visible, kept_lse, context_grad = inputs
    query_heads = split_heads(query_rows)
    key_heads = split_heads(key_rows)
    value_heads = split_heads(value_rows)
    grad_heads = split_heads(context_grad)
    probs = jnp.exp(masked_scores(query_heads, key_heads, visible) - kept_lse)
    prob_grad = jnp.einsum(
        "qhd,khd->hqk", grad_heads, value_heads, preferred_element_type=jnp.float32
    )
    centered = prob_grad - jnp.sum(prob_grad * probs, axis=-1, keepdims=True)
    score_grad = (probs * centered).astype(jnp.bfloat16)
    query_grad = (
        jnp.einsum("hqk,khd->qhd", score_grad, key_heads, preferred_element_type=jnp.float32)
        * scaling
    )
    key_grad = (
        jnp.einsum("hqk,qhd->khd", score_grad, query_heads, preferred_element_type=jnp.float32)
        * scaling
    )
    value_grad = jnp.einsum(
        "hqk,qhd->khd", probs.astype(jnp.bfloat16), grad_heads, preferred_element_type=jnp.float32
    )
    return (
        query_grad.reshape(query_rows.shape),
        key_grad.reshape(key_rows.shape),
        value_grad.reshape(value_rows.shape),
    )


def on_device(
    token_ids,
    lengths,
    word_table,
    position_table,
    embed_gain,
    embed_bias,
    query_weight,
    query_bias,
    key_weight,
    value_weight,
    value_bias,
    output_weight,
    output_bias,
    middle_gain,
    middle_bias,
    inner_weight,
    inner_bias,
    outer_weight,
    outer_bias,
    final_gain,
    final_bias,
    cotangent,
):
    gathered = (
        lax.all_gather(position_table, "vocab", axis=0, tiled=True),
        lax.all_gather(embed_gain, "vocab", axis=0, tiled=True),
        lax.all_gather(embed_bias, "vocab", axis=0, tiled=True),
        lax.all_gather(query_weight, "vocab", axis=0, tiled=True),
        lax.all_gather(query_bias, "vocab", axis=0, tiled=True),
        lax.all_gather(key_weight, "vocab", axis=0, tiled=True),
        lax.all_gather(value_weight, "vocab", axis=0, tiled=True),
        lax.all_gather(value_bias, "vocab", axis=0, tiled=True),
        lax.all_gather(output_weight, "vocab", axis=0, tiled=True),
        lax.all_gather(output_bias, "vocab", axis=0, tiled=True),
        lax.all_gather(middle_gain, "vocab", axis=0, tiled=True),
        lax.all_gather(middle_bias, "vocab", axis=0, tiled=True),
        lax.all_gather(inner_weight, "vocab", axis=0, tiled=True),
        lax.all_gather(inner_bias, "vocab", axis=0, tiled=True),
        lax.all_gather(outer_weight, "vocab", axis=0, tiled=True),
        lax.all_gather(outer_bias, "vocab", axis=0, tiled=True),
        lax.all_gather(final_gain, "vocab", axis=0, tiled=True),
        lax.all_gather(final_bias, "vocab", axis=0, tiled=True),
    )
    (
        position_rows,
        embed_scale,
        embed_shift,
        query_matrix,
        query_shift,
        key_matrix,
        value_matrix,
        value_shift,
        output_matrix,
        output_shift,
        middle_scale,
        middle_shift,
        inner_matrix,
        inner_shift,
        outer_matrix,
        outer_shift,
        final_scale,
        final_shift,
    ) = gathered
    seq_here, full_len = token_ids.shape
    table_rows, width = word_table.shape
    tok_rows = seq_here * full_len
    vocab_index = lax.axis_index("vocab")
    table_start = vocab_index * table_rows
    table_cols = table_start + lax.iota(jnp.int32, table_rows)
    group_ids = lax.all_gather(token_ids, "vocab", axis=0, tiled=True).reshape(-1)
    id_part = group_ids - table_start
    inside = (id_part >= 0) & (id_part < table_rows)
    picked = jnp.take(word_table, jnp.clip(id_part, 0, table_rows - 1), axis=0)
    embedded = lax.psum_scatter(
        jnp.where(inside[:, None], picked.astype(jnp.float32), 0.0).astype(jnp.bfloat16),
        "vocab",
        scatter_dimension=0,
        tiled=True,
    ).astype(jnp.float32)
    place_rows = position_rows.astype(jnp.float32)
    summed = (embedded.reshape(seq_here, full_len, width) + place_rows[None]).reshape(
        tok_rows, width
    )
    normed, hat_embed, inv_embed = normalize(
        summed, embed_scale.astype(jnp.float32), embed_shift.astype(jnp.float32)
    )
    normed_low = normed.astype(jnp.bfloat16)
    query_low = (matmul(normed_low, query_matrix) + query_shift.astype(jnp.float32)).astype(
        jnp.bfloat16
    )
    key_low = matmul(normed_low, key_matrix).astype(jnp.bfloat16)
    value_low = (matmul(normed_low, value_matrix) + value_shift.astype(jnp.float32)).astype(
        jnp.bfloat16
    )
    visible = lax.iota(jnp.int32, full_len)[None, :] < lengths[:, None]
    query_seq = query_low.reshape(seq_here, full_len, width)
    key_full = key_low.reshape(seq_here, full_len, width)
    value_full = value_low.reshape(seq_here, full_len, width)
    context, lse_kept = lax.map(attend, (query_seq, key_full, value_full, visible))
    context = context.reshape(tok_rows, width)
    attended = matmul(context, output_matrix) + output_shift.astype(jnp.float32)
    middle, hat_middle, inv_middle = normalize(
        normed + attended, middle_scale.astype(jnp.float32), middle_shift.astype(jnp.float32)
    )
    middle_low = middle.astype(jnp.bfloat16)
    inner = matmul(middle_low, inner_matrix) + inner_shift.astype(jnp.float32)
    activated = jax.nn.gelu(inner, approximate=False).astype(jnp.bfloat16)
    branch = matmul(activated, outer_matrix) + outer_shift.astype(jnp.float32)
    result, hat_final, inv_final = normalize(
        middle + branch, final_scale.astype(jnp.float32), final_shift.astype(jnp.float32)
    )
    output = result.astype(jnp.bfloat16).reshape(seq_here, full_len, width)
    (
        embed_scale,
        query_matrix,
        key_matrix,
        value_matrix,
        output_matrix,
        middle_scale,
        inner_matrix,
        outer_matrix,
        final_scale,
    ) = (
        lax.all_gather(embed_gain, "vocab", axis=0, tiled=True),
        lax.all_gather(query_weight, "vocab", axis=0, tiled=True),
        lax.all_gather(key_weight, "vocab", axis=0, tiled=True),
        lax.all_gather(value_weight, "vocab", axis=0, tiled=True),
        lax.all_gather(output_weight, "vocab", axis=0, tiled=True),
        lax.all_gather(middle_gain, "vocab", axis=0, tiled=True),
        lax.all_gather(inner_weight, "vocab", axis=0, tiled=True),
        lax.all_gather(outer_weight, "vocab", axis=0, tiled=True),
        lax.all_gather(final_gain, "vocab", axis=0, tiled=True),
    )
    upstream = cotangent.reshape(tok_rows, width).astype(jnp.float32)
    final_gain_gradient = jnp.sum(upstream * hat_final, axis=0)
    final_bias_gradient = jnp.sum(upstream, axis=0)
    second = normalize_back(upstream, hat_final, inv_final, final_scale.astype(jnp.float32))
    branch_grad = second.astype(jnp.bfloat16)
    outer_bias_gradient = jnp.sum(branch_grad.astype(jnp.float32), axis=0)
    outer_weight_gradient = contract_rows(activated, branch_grad)
    inner_grad = (times_transposed(branch_grad, outer_matrix) * gelu_slope(inner)).astype(
        jnp.bfloat16
    )
    inner_bias_gradient = jnp.sum(inner_grad.astype(jnp.float32), axis=0)
    inner_weight_gradient = contract_rows(middle_low, inner_grad)
    middle_grad = second + times_transposed(inner_grad, inner_matrix)
    middle_gain_gradient = jnp.sum(middle_grad * hat_middle, axis=0)
    middle_bias_gradient = jnp.sum(middle_grad, axis=0)
    first = normalize_back(middle_grad, hat_middle, inv_middle, middle_scale.astype(jnp.float32))
    attended_grad = first.astype(jnp.bfloat16)
    output_bias_gradient = jnp.sum(attended_grad.astype(jnp.float32), axis=0)
    output_weight_gradient = contract_rows(context, attended_grad)
    context_grad = times_transposed(attended_grad, output_matrix).astype(jnp.bfloat16)
    context_grad = context_grad.reshape(seq_here, full_len, width)
    query_grad, key_grad, value_grad = lax.map(
        attend_back, (query_seq, key_full, value_full, visible, lse_kept, context_grad)
    )
    query_low_grad = query_grad.reshape(tok_rows, width).astype(jnp.bfloat16)
    key_low_grad = key_grad.reshape(tok_rows, width).astype(jnp.bfloat16)
    value_low_grad = value_grad.reshape(tok_rows, width).astype(jnp.bfloat16)
    query_bias_gradient = jnp.sum(query_low_grad.astype(jnp.float32), axis=0)
    value_bias_gradient = jnp.sum(value_low_grad.astype(jnp.float32), axis=0)
    query_weight_gradient = contract_rows(normed_low, query_low_grad)
    key_weight_gradient = contract_rows(normed_low, key_low_grad)
    value_weight_gradient = contract_rows(normed_low, value_low_grad)
    normed_grad = (
        first
        + times_transposed(query_low_grad, query_matrix)
        + times_transposed(key_low_grad, key_matrix)
        + times_transposed(value_low_grad, value_matrix)
    )
    embed_gain_gradient = jnp.sum(normed_grad * hat_embed, axis=0)
    embed_bias_gradient = jnp.sum(normed_grad, axis=0)
    summed_grad = normalize_back(normed_grad, hat_embed, inv_embed, embed_scale.astype(jnp.float32))
    position_gradient = jnp.sum(summed_grad.reshape(seq_here, full_len, width), axis=0)
    embedded_grad = summed_grad.astype(jnp.bfloat16)

    def table_term(id_block, grad_block):
        onehot = (id_block[:, None] == table_cols[None, :]).astype(jnp.bfloat16)
        return jnp.einsum("tv,td->vd", onehot, grad_block, preferred_element_type=jnp.float32)

    running = jnp.zeros((table_rows, width), jnp.float32)
    portion = lax.all_gather(embedded_grad, "vocab", axis=0, tiled=True)
    number = portion.shape[0]
    id_part = group_ids

    def step(carry, pieces):
        return (carry + table_term(pieces[0], pieces[1]), None)

    running, unused = lax.scan(
        step,
        running,
        (
            id_part.reshape(number // tok_rows, tok_rows),
            portion.reshape(number // tok_rows, tok_rows, width),
        ),
    )
    shares = (
        lax.psum_scatter(
            position_gradient.astype(jnp.bfloat16), "vocab", scatter_dimension=0, tiled=True
        ).astype(jnp.float32),
        lax.psum_scatter(
            embed_gain_gradient.astype(jnp.bfloat16), "vocab", scatter_dimension=0, tiled=True
        ).astype(jnp.float32),
        lax.psum_scatter(
            embed_bias_gradient.astype(jnp.bfloat16), "vocab", scatter_dimension=0, tiled=True
        ).astype(jnp.float32),
        lax.psum_scatter(
            query_weight_gradient.astype(jnp.bfloat16), "vocab", scatter_dimension=0, tiled=True
        ).astype(jnp.float32),
        lax.psum_scatter(
            query_bias_gradient.astype(jnp.bfloat16), "vocab", scatter_dimension=0, tiled=True
        ).astype(jnp.float32),
        lax.psum_scatter(
            key_weight_gradient.astype(jnp.bfloat16), "vocab", scatter_dimension=0, tiled=True
        ).astype(jnp.float32),
        lax.psum_scatter(
            value_weight_gradient.astype(jnp.bfloat16), "vocab", scatter_dimension=0, tiled=True
        ).astype(jnp.float32),
        lax.psum_scatter(
            value_bias_gradient.astype(jnp.bfloat16), "vocab", scatter_dimension=0, tiled=True
        ).astype(jnp.float32),
        lax.psum_scatter(
            output_weight_gradient.astype(jnp.bfloat16), "vocab", scatter_dimension=0, tiled=True
        ).astype(jnp.float32),
        lax.psum_scatter(
            output_bias_gradient.astype(jnp.bfloat16), "vocab", scatter_dimension=0, tiled=True
        ).astype(jnp.float32),
        lax.psum_scatter(
            middle_gain_gradient.astype(jnp.bfloat16), "vocab", scatter_dimension=0, tiled=True
        ).astype(jnp.float32),
        lax.psum_scatter(
            middle_bias_gradient.astype(jnp.bfloat16), "vocab", scatter_dimension=0, tiled=True
        ).astype(jnp.float32),
        lax.psum_scatter(
            inner_weight_gradient.astype(jnp.bfloat16), "vocab", scatter_dimension=0, tiled=True
        ).astype(jnp.float32),
        lax.psum_scatter(
            inner_bias_gradient.astype(jnp.bfloat16), "vocab", scatter_dimension=0, tiled=True
        ).astype(jnp.float32),
        lax.psum_scatter(
            outer_weight_gradient.astype(jnp.bfloat16), "vocab", scatter_dimension=0, tiled=True
        ).astype(jnp.float32),
        lax.psum_scatter(
            outer_bias_gradient.astype(jnp.bfloat16), "vocab", scatter_dimension=0, tiled=True
        ).astype(jnp.float32),
        lax.psum_scatter(
            final_gain_gradient.astype(jnp.bfloat16), "vocab", scatter_dimension=0, tiled=True
        ).astype(jnp.float32),
        lax.psum_scatter(
            final_bias_gradient.astype(jnp.bfloat16), "vocab", scatter_dimension=0, tiled=True
        ).astype(jnp.float32),
    )
    totals = (
        lax.psum(running.astype(jnp.bfloat16), "dp").astype(jnp.float32),
        lax.psum(shares[0].astype(jnp.bfloat16), "dp").astype(jnp.float32),
        lax.psum(shares[1].astype(jnp.bfloat16), "dp").astype(jnp.float32),
        lax.psum(shares[2].astype(jnp.bfloat16), "dp").astype(jnp.float32),
        lax.psum(shares[3].astype(jnp.bfloat16), "dp").astype(jnp.float32),
        lax.psum(shares[4].astype(jnp.bfloat16), "dp").astype(jnp.float32),
        lax.psum(shares[5].astype(jnp.bfloat16), "dp").astype(jnp.float32),
        lax.psum(shares[6].astype(jnp.bfloat16), "dp").astype(jnp.float32),
        lax.psum(shares[7].astype(jnp.bfloat16), "dp").astype(jnp.float32),
        lax.psum(shares[8].astype(jnp.bfloat16), "dp").astype(jnp.float32),
        lax.psum(shares[9].astype(jnp.bfloat16), "dp").astype(jnp.float32),
        lax.psum(shares[10].astype(jnp.bfloat16), "dp").astype(jnp.float32),
        lax.psum(shares[11].astype(jnp.bfloat16), "dp").astype(jnp.float32),
        lax.psum(shares[12].astype(jnp.bfloat16), "dp").astype(jnp.float32),
        lax.psum(shares[13].astype(jnp.bfloat16), "dp").astype(jnp.float32),
        lax.psum(shares[14].astype(jnp.bfloat16), "dp").astype(jnp.float32),
        lax.psum(shares[15].astype(jnp.bfloat16), "dp").astype(jnp.float32),
        lax.psum(shares[16].astype(jnp.bfloat16), "dp").astype(jnp.float32),
        lax.psum(shares[17].astype(jnp.bfloat16), "dp").astype(jnp.float32),
    )
    return (
        output,
        totals[0],
        totals[1],
        totals[2],
        totals[3],
        totals[4],
        totals[5],
        totals[6],
        totals[7],
        totals[8],
        totals[9],
        totals[10],
        totals[11],
        totals[12],
        totals[13],
        totals[14],
        totals[15],
        totals[16],
        totals[17],
        totals[18],
    )


def solution(mesh):
    return jax.shard_map(
        on_device,
        mesh=mesh,
        in_specs=(
            P(("dp", "vocab"), None),
            P(("dp", "vocab")),
            P("vocab", None),
            P("vocab", None),
            P("vocab"),
            P("vocab"),
            P("vocab", None),
            P("vocab"),
            P("vocab", None),
            P("vocab", None),
            P("vocab"),
            P("vocab", None),
            P("vocab"),
            P("vocab"),
            P("vocab"),
            P("vocab", None),
            P("vocab"),
            P("vocab", None),
            P("vocab"),
            P("vocab"),
            P("vocab"),
            P(("dp", "vocab"), None, None),
        ),
        out_specs=(
            P(("dp", "vocab"), None, None),
            P("vocab", None),
            P("vocab", None),
            P("vocab"),
            P("vocab"),
            P("vocab", None),
            P("vocab"),
            P("vocab", None),
            P("vocab", None),
            P("vocab"),
            P("vocab", None),
            P("vocab"),
            P("vocab"),
            P("vocab"),
            P("vocab", None),
            P("vocab"),
            P("vocab", None),
            P("vocab"),
            P("vocab"),
            P("vocab"),
        ),
        check_vma=False,
    )
```

profile of v0, /device:TPU:0, one launch (start us, length us, event | category | flops | bytes accessed | tf_op | source)
XLA Modules:
  0.0 1373.0 jit_solution(14614542434230995615)
XLA Ops:
  7.2 28.1 %all-gather = s32[8,1,512]{2,1,0:T(1,128)S(1)} all-gather(s32[1,1,512]{2,1,0:T(1,128)} %bitcast.130), channel_id=1, replica_groups=mesh['dp'=4,'vocab'=8] {'vocab'}, dimensions={0}, use_global_device_ids=true | all-gather | bytes 18432 | tf_op jit(solution)/shard_map/all_gather | solution.py:178
  35.5 22.5 %gather_fusion = bf16[4096,768]{1,0:T(8,128)(2,1)} fusion(bf16[3840,768]{1,0:T(8,128)(2,1)} %param.26, s32[4096]{0:T(1024)S(1)} %broadcast_clamp_fusion), kind=kCustom, calls=%fused_computation | custom fusion | bytes 12599296 | tf_op jit(solution)/shard_map/jit(_take)/gather | solution.py:181
  73.6 37.5 %all-reduce.22 = (bf16[768]{0:T(1024)(128)(2,1)S(1)}, bf16[768]{0:T(1024)(128)(2,1)S(1)}, bf16[768]{0:T(1024)(128)(2,1)S(1)}, bf16[768]{0:T(1024)(128)(2,1)S(1)}...) all-reduce(bf16[768]{0:T(1024)(128)(2,1)S(1)} %dynamic-update-slice, ...), channel_id=1, replica_groups=mesh['dp'=4,'vocab'=8] {'vocab'}, use_global_device_ids=true, to_apply=%add.1 | all-reduce | flops 6912 | bytes 27648
  111.1 33.9 %all_gather.70 = bf16[512,768]{1,0:T(8,128)(2,1)S(1)} all-gather(bf16[64,768]{1,0:T(8,128)(2,1)S(1)} %copy-done.32), channel_id=1, replica_groups=mesh['dp'=4,'vocab'=8] {'vocab'}, dimensions={0}, use_global_device_ids=true | all-gather | bytes 884736 | tf_op jit(solution)/shard_map/all_gather | solution.py:133
  145.8 26.6 %all-gather.1 = bf16[8,1,384]{2,1,0:T(2,128)(2,1)S(1)} all-gather(bf16[1,1,384]{2,1,0:T(2,128)(2,1)S(1)} %reshape.397), channel_id=1, replica_groups=mesh['dp'=4,'vocab'=8] {'vocab'}, dimensions={0}, use_global_device_ids=true | all-gather | bytes 6912 | tf_op jit(solution)/shard_map/all_gather | solution.py:146
  172.4 20.5 %reduce-scatter.9.cloned.1.call-done = bf16[512,768]{1,0:T(8,128)(2,1)} async-done(((bf16[4096,768]{1,0:T(8,128)(2,1)}), bf16[512,768]{1,0:T(8,128)(2,1)}) %reduce-scatter.9.cloned.1.call-update) | async-done | bytes 786448 | tf_op jit(solution)/shard_map/reduce_scatter | solution.py:182
  195.3 40.3 %all-gather.12.cloned.1.call-done = bf16[768,768]{1,0:T(8,128)(2,1)} async-done(((bf16[96,768]{1,0:T(8,128)(2,1)}), bf16[768,768]{1,0:T(8,128)(2,1)}) %all-gather.12.cloned.1.call-update) | async-done | bytes 1179664 | tf_op jit(solution)/shard_map/all_gather | solution.py:136
  237.9 39.7 %all-gather.14.cloned.1.call-done = bf16[768,768]{1,0:T(8,128)(2,1)} async-done(((bf16[96,768]{1,0:T(8,128)(2,1)}), bf16[768,768]{1,0:T(8,128)(2,1)}) %all-gather.14.cloned.1.call-update) | async-done | bytes 1179664 | tf_op jit(solution)/shard_map/all_gather | solution.py:138
  282.1 37.3 %all-gather.10.cloned.1.call-done = bf16[768,768]{1,0:T(8,128)(2,1)} async-done(((bf16[96,768]{1,0:T(8,128)(2,1)}), bf16[768,768]{1,0:T(8,128)(2,1)}) %all-gather.10.cloned.1.call-update) | async-done | bytes 1179664 | tf_op jit(solution)/shard_map/all_gather | solution.py:139
  336.0 25.3 %all-gather.16.cloned.1.call-done = bf16[768,768]{1,0:T(8,128)(2,1)} async-done(((bf16[96,768]{1,0:T(8,128)(2,1)}), bf16[768,768]{1,0:T(8,128)(2,1)}) %all-gather.16.cloned.1.call-update) | async-done | bytes 1179664 | tf_op jit(solution)/shard_map/all_gather | solution.py:141
  364.3 77.1 %all-gather.18.cloned.1.call-done = bf16[768,3072]{1,0:T(8,128)(2,1)} async-done(((bf16[96,3072]{1,0:T(8,128)(2,1)}), bf16[768,3072]{1,0:T(8,128)(2,1)}) %all-gather.18.cloned.1.call-update) | async-done | bytes 4718608 | tf_op jit(solution)/shard_map/all_gather | solution.py:145
  441.4 19.1 %fusion.15 = (bf16[512,3072]{1,0:T(8,128)(2,1)}, f32[512,3072]{1,0:T(8,128)}) fusion(f32[3072]{0:T(1024)S(1)} %bitcast.128, bf16[768,3072]{1,0:T(8,128)(2,1)} %all-gather.18.cloned.1.call-done, f32[512,768]{1,0:T(8,128)S(1)} %get-tuple-element.192, f32[768]{0:T(1024)S(1)} %convert_element_type.311, f32[768]{0:T(1024)S(1)} %convert_element_type.310, ...), kind=kOutput, calls=%fused_computation.25 | convolution fusion | flops 2521694208 | bytes 15751168 | tf_op jit(solution)/shard_map/dot_general | solution.py:38
  460.5 60.8 %all-gather.20.cloned.1.call-done = bf16[3072,768]{1,0:T(8,128)(2,1)} async-done(((bf16[384,768]{1,0:T(8,128)(2,1)}), bf16[3072,768]{1,0:T(8,128)(2,1)}) %all-gather.20.cloned.1.call-update) | async-done | bytes 4718608 | tf_op jit(solution)/shard_map/all_gather | solution.py:147
  545.6 12.2 multiply_reduce_fusion
  605.6 68.3 %all-gather.22.cloned.1.call-done = bf16[4096,768]{1,0:T(8,128)(2,1)} async-done(((bf16[512,768]{1,0:T(8,128)(2,1)}), bf16[4096,768]{1,0:T(8,128)(2,1)}) %all-gather.22.cloned.1.call-update) | async-done | bytes 6291472 | tf_op jit(solution)/shard_map/all_gather | solution.py:291
  673.9 72.4 %while.3 = (s32[]{:T(128)}, f32[3840,768]{1,0:T(8,128)}, s32[8,512]{1,0:T(8,128)S(1)}, bf16[8,512,768]{2,1,0:T(8,128)(2,1)}, s32[]{:T(128)}, /*index=5*/s32[]{:T(128)}, s32[]{:T(128)}) while((s32[]{:T(128)}, f32[3840,768]{1,0:T(8,128)}, s32[8,512]{1,0:T(8,128)S(1)}, bf16[8,512,768]{2,1,0:T(8,128)(2,1)}, s32[]{:T(128)}, ...), condition=%wide.region_17.18_spmd.clone, body=%wide.region_16.17_spmd.clone.sunk | while | flops 3027767040 | bytes 24416860 | solution.py:298
  753.9 52.6 %reduce-scatter.13.cloned.1.call-done = bf16[96,768]{1,0:T(8,128)(2,1)} async-done(((bf16[768,768]{1,0:T(8,128)(2,1)}), bf16[96,768]{1,0:T(8,128)(2,1)}) %reduce-scatter.13.cloned.1.call-update) | async-done | bytes 147472 | tf_op jit(solution)/shard_map/reduce_scatter | solution.py:316
  806.6 67.8 %reduce-scatter.15.cloned.1.call-done = bf16[96,768]{1,0:T(8,128)(2,1)} async-done(((bf16[768,768]{1,0:T(8,128)(2,1)}), bf16[96,768]{1,0:T(8,128)(2,1)}) %reduce-scatter.15.cloned.1.call-update) | async-done | bytes 147472 | tf_op jit(solution)/shard_map/reduce_scatter | solution.py:322
  874.4 67.2 %reduce-scatter.19.cloned.1.call-done = bf16[96,768]{1,0:T(8,128)(2,1)} async-done(((bf16[768,768]{1,0:T(8,128)(2,1)}), bf16[96,768]{1,0:T(8,128)(2,1)}) %reduce-scatter.19.cloned.1.call-update) | async-done | bytes 147472 | tf_op jit(solution)/shard_map/reduce_scatter | solution.py:331
  941.5 67.3 %reduce-scatter.17.cloned.1.call-done = bf16[96,768]{1,0:T(8,128)(2,1)} async-done(((bf16[768,768]{1,0:T(8,128)(2,1)}), bf16[96,768]{1,0:T(8,128)(2,1)}) %reduce-scatter.17.cloned.1.call-update) | async-done | bytes 147472 | tf_op jit(solution)/shard_map/reduce_scatter | solution.py:325
  1008.8 98.2 %reduce-scatter.21.cloned.1.call-done = bf16[96,3072]{1,0:T(8,128)(2,1)} async-done(((bf16[768,3072]{1,0:T(8,128)(2,1)}), bf16[96,3072]{1,0:T(8,128)(2,1)}) %reduce-scatter.21.cloned.1.call-update) | async-done | bytes 589840 | tf_op jit(solution)/shard_map/reduce_scatter | solution.py:343
  1107.1 98.8 %reduce-scatter.23.cloned.1.call-done = bf16[384,768]{1,0:T(8,128)(2,1)} async-done(((bf16[3072,768]{1,0:T(8,128)(2,1)}), bf16[384,768]{1,0:T(8,128)(2,1)}) %reduce-scatter.23.cloned.1.call-update) | async-done | bytes 589840 | tf_op jit(solution)/shard_map/reduce_scatter | solution.py:349
  1208.9 35.8 %all-reduce.21 = (bf16[768]{0:T(1024)(128)(2,1)S(1)}, bf16[768]{0:T(1024)(128)(2,1)S(1)}, bf16[768]{0:T(1024)(128)(2,1)S(1)}, bf16[768]{0:T(1024)(128)(2,1)S(1)}...) all-reduce(bf16[768]{0:T(1024)(128)(2,1)S(1)} %dynamic-update-slice, ...), channel_id=1, replica_groups=mesh['dp'=4,'vocab'=8] {'vocab'}, use_global_device_ids=true, to_apply=%add.9 | all-reduce | flops 11520 | bytes 46080
  1259.2 92.9 %all-reduce.27.cloned.1.call-done = (bf16[3840,768]{1,0:T(8,128)(2,1)}, bf16[64,768]{1,0:T(8,128)(2,1)}, bf16[96,768]{1,0:T(8,128)(2,1)}, bf16[96,768]{1,0:T(8,1...) async-done(((bf16[3840,768]{1,0:T(8,128)(2,1)}, bf16[64,768]{1,0:T(8,128)(2,1)}, ...) | async-done | bytes 7766032 | tf_op jit(solution)/shard_map/psum | solution.py:363
  (303 shorter events, 225.5 us)
Async XLA Ops:
  7.2 185.7 %reduce-scatter.9.cloned.1.call-start = ((), (), s32[]{:S(2)}) async-start(), calls=%async_computation.8 | async-start | bytes 7077888 | tf_op jit(solution)/shard_map/reduce_scatter | solution.py:182
  35.3 22.6 %copy-start.26 = (s32[8,1,512]{2,1,0:T(1,128)}, s32[8,1,512]{2,1,0:T(1,128)S(1)}, u32[]{:S(2)}) copy-start(s32[8,1,512]{2,1,0:T(1,128)S(1)} %all-gather) | copy-start | bytes 49156
  66.2 45.0 %copy-start.32 = (bf16[64,768]{1,0:T(8,128)(2,1)S(1)}, bf16[64,768]{1,0:T(8,128)(2,1)}, u32[]{:S(2)}) copy-start(bf16[64,768]{1,0:T(8,128)(2,1)} %param.27) | copy-start | bytes 294916
  66.2 79.6 %copy-start.35 = (bf16[384]{0:T(512)(128)(2,1)S(1)}, bf16[384]{0:T(512)(128)(2,1)}, u32[]{:S(2)}) copy-start(bf16[384]{0:T(512)(128)(2,1)} %param.40) | copy-start | bytes 2308
  66.2 169.3 %all-gather.12.cloned.1.call-start = ((), (), s32[]{:S(2)}) async-start(), calls=%async_computation.10 | async-start | bytes 1327104 | tf_op jit(solution)/shard_map/all_gather | solution.py:136
  66.9 210.6 %all-gather.14.cloned.1.call-start = ((), (), s32[]{:S(2)}) async-start(), calls=%async_computation.11 | async-start | bytes 1327104 | tf_op jit(solution)/shard_map/all_gather | solution.py:138
  67.7 251.8 %all-gather.10.cloned.1.call-start = ((), (), s32[]{:S(2)}) async-start(), calls=%async_computation.9 | async-start | bytes 1327104 | tf_op jit(solution)/shard_map/all_gather | solution.py:139
  68.2 293.1 %all-gather.16.cloned.1.call-start = ((), (), s32[]{:S(2)}) async-start(), calls=%async_computation.12 | async-start | bytes 1327104 | tf_op jit(solution)/shard_map/all_gather | solution.py:141
  68.8 372.6 %all-gather.18.cloned.1.call-start = ((), (), s32[]{:S(2)}) async-start(), calls=%async_computation.13 | async-start | bytes 5308416 | tf_op jit(solution)/shard_map/all_gather | solution.py:145
  69.4 451.9 %all-gather.20.cloned.1.call-start = ((), (), s32[]{:S(2)}) async-start(), calls=%async_computation.14 | async-start | bytes 5308416 | tf_op jit(solution)/shard_map/all_gather | solution.py:147
  70.2 603.8 %all-gather.22.cloned.1.call-start = ((), (), s32[]{:S(2)}) async-start(), calls=%async_computation.15 | async-start | bytes 7077888 | tf_op jit(solution)/shard_map/all_gather | solution.py:291
  195.3 40.3 %copy-start.21 = (bf16[512,768]{1,0:T(8,128)(2,1)}, bf16[512,768]{1,0:T(8,128)(2,1)S(1)}, u32[]{:S(2)}) copy-start(bf16[512,768]{1,0:T(8,128)(2,1)S(1)} %fusion.47) | copy-start | bytes 2359300
  237.9 87.0 %copy-start.9 = (bf16[512,768]{0,1:T(8,128)(2,1)}, bf16[512,768]{0,1:T(8,128)(2,1)S(1)}, u32[]{:S(2)}) copy-start(bf16[512,768]{0,1:T(8,128)(2,1)S(1)} %copy.63) | copy-start | bytes 2359300
  282.1 42.8 %copy-start.4 = (bf16[512,768]{0,1:T(8,128)(2,1)}, bf16[512,768]{0,1:T(8,128)(2,1)S(1)}, u32[]{:S(2)}) copy-start(bf16[512,768]{0,1:T(8,128)(2,1)S(1)} %copy.64) | copy-start | bytes 2359300
  363.9 96.5 %copy-start.11 = (f32[512,768]{1,0:T(8,128)}, f32[512,768]{1,0:T(8,128)S(1)}, u32[]{:S(2)}) copy-start(f32[512,768]{1,0:T(8,128)S(1)} %get-tuple-element.192) | copy-start | bytes 4718596
  545.6 12.2 slice-start.2
  576.7 177.2 %reduce-scatter.11.cloned.1.call-start = ((), (), s32[]{:S(2)}) async-start(), calls=%async_computation.16 | async-start | bytes 884736 | tf_op jit(solution)/shard_map/reduce_scatter | solution.py:307
  577.5 229.1 %reduce-scatter.13.cloned.1.call-start = ((), (), s32[]{:S(2)}) async-start(), calls=%async_computation.17 | async-start | bytes 1327104 | tf_op jit(solution)/shard_map/reduce_scatter | solution.py:316
  580.0 294.4 %reduce-scatter.15.cloned.1.call-start = ((), (), s32[]{:S(2)}) async-start(), calls=%async_computation.18 | async-start | bytes 1327104 | tf_op jit(solution)/shard_map/reduce_scatter | solution.py:322
  583.3 358.2 %reduce-scatter.19.cloned.1.call-start = ((), (), s32[]{:S(2)}) async-start(), calls=%async_computation.20 | async-start | bytes 1327104 | tf_op jit(solution)/shard_map/reduce_scatter | solution.py:331
  586.7 422.1 %reduce-scatter.17.cloned.1.call-start = ((), (), s32[]{:S(2)}) async-start(), calls=%async_computation.19 | async-start | bytes 1327104 | tf_op jit(solution)/shard_map/reduce_scatter | solution.py:325
  589.8 517.2 %reduce-scatter.21.cloned.1.call-start = ((), (), s32[]{:S(2)}) async-start(), calls=%async_computation.21 | async-start | bytes 5308416 | tf_op jit(solution)/shard_map/reduce_scatter | solution.py:343
  597.6 608.3 %reduce-scatter.23.cloned.1.call-start = ((), (), s32[]{:S(2)}) async-start(), calls=%async_computation.22 | async-start | bytes 5308416 | tf_op jit(solution)/shard_map/reduce_scatter | solution.py:349
  605.6 746.6 %all-reduce.27.cloned.1.call-start = ((), (), s32[]{:S(2)}) async-start(), calls=%async_computation.23 | async-start | bytes 15532032 | tf_op jit(solution)/shard_map/psum | solution.py:363
  (49 other events, 203.7 us)
Sparse Core Ops, SparseCore 0:
  66.2 126.7 reduce-scatter.8
  195.1 40.3 all-gather.11
  237.7 39.7 all-gather.13
  279.6 39.7 all-gather.9
  321.5 39.8 all-gather.15
  363.3 78.0 all-gather.17
  443.6 77.6 all-gather.19
  576.9 97.0 all-gather.21
  677.2 61.4 reduce-scatter.10
  742.6 63.9 reduce-scatter.12
  810.5 63.8 reduce-scatter.14
  877.6 63.8 reduce-scatter.18
  944.9 63.8 reduce-scatter.16
  1012.3 94.6 reduce-scatter.20
  1110.5 95.3 reduce-scatter.22
  1208.6 143.5 all-reduce.26
where the time goes:
time: 1380 us; the launch traced here: 1370 us
  waiting for transfers between devices  919 us (67%)
  matrix products  172 us (12%)
  blocking collectives  169 us (12%)
  other arithmetic  52 us (4%)
  local copies, waits for them, and re-layouts  42.7 us (3%)
  between operations  17.6 us (1%)
    reduce_scatter x1, waiting for transfers between devices, on_device(): lax.psum_scatter(outer_weight_gradient.astype(jnp.bfloat16), 'vocab', sca...  98.8 us
    reduce_scatter x1, waiting for transfers between devices, on_device(): lax.psum_scatter(inner_weight_gradient.astype(jnp.bfloat16), 'vocab', sca...  98.2 us
    psum x1, waiting for transfers between devices, on_device(): lax.psum(running.astype(jnp.bfloat16), 'dp').astype(jnp.float32)  92.9 us
    all_gather x1, waiting for transfers between devices, on_device(): lax.all_gather(inner_weight, 'vocab', axis=0, tiled=True)  77.1 us
    unnamed x2, blocking collectives  73.3 us
    dot_general x8, matrix products, table_term(): jnp.einsum('tv,td->vd', onehot, grad_block, preferred_element_type=jnp.fl...  72.3 us
    all_gather x1, waiting for transfers between devices, on_device(): portion = lax.all_gather(embedded_grad, 'vocab', axis=0, tiled=True)  68.3 us
    reduce_scatter x1, waiting for transfers between devices, on_device(): lax.psum_scatter(key_weight_gradient.astype(jnp.bfloat16), 'vocab', scatt...  67.8 us
  transfers between devices with their start and end apart: 16, of which 15 were waited for; matrix products, arithmetic and copies ran while one was open for 12% of the time, Pallas kernels for 0%

commit v1 on v0

v1 whole, which is shorter than its diff:
```python
import functools
import math

import jax
import jax.numpy as jnp
from jax import lax
from jax.sharding import PartitionSpec as P

HEADS = 12


epsilon = 1e-12
scaling = 0.125


def normalize(values, gain, bias_row):
    center = values - jnp.mean(values, axis=-1, keepdims=True)
    inverse = lax.rsqrt(jnp.mean(center * center, axis=-1, keepdims=True) + epsilon)
    scaled = center * inverse
    return (scaled * gain + bias_row, scaled, inverse)


def normalize_back(upstream, scaled, inverse, gain):
    weighted = upstream * gain
    return inverse * (
        weighted
        - jnp.mean(weighted, axis=-1, keepdims=True)
        - scaled * jnp.mean(weighted * scaled, axis=-1, keepdims=True)
    )


def gelu_slope(inner):
    cumulative = 0.5 * (1.0 + lax.erf(inner * (1.0 / math.sqrt(2.0))))
    density = jnp.exp(-0.5 * inner * inner) * (1.0 / math.sqrt(2.0 * math.pi))
    return cumulative + inner * density


def matmul(left, right):
    return jnp.dot(left, right, preferred_element_type=jnp.float32)


def contract_rows(left, right):
    return jnp.einsum("ti,tj->ij", left, right, preferred_element_type=jnp.float32)


def times_transposed(left, right):
    return jnp.einsum("tj,ij->ti", left, right, preferred_element_type=jnp.float32)


def split_heads(rows):
    return rows.reshape(rows.shape[0], HEADS, rows.shape[1] // HEADS)


def masked_scores(query_heads, key_heads, visible):
    scores = (
        jnp.einsum("qhd,khd->hqk", query_heads, key_heads, preferred_element_type=jnp.float32)
        * scaling
    )
    return jnp.where(visible[None, None, :], scores, -1e30)


def attend(inputs):
    query_rows, key_rows, value_rows, visible = inputs
    query_heads = split_heads(query_rows)
    scores = masked_scores(query_heads, split_heads(key_rows), visible)
    largest = jnp.max(scores, axis=-1, keepdims=True)
    raised = jnp.exp(scores - largest)
    totals = jnp.sum(raised, axis=-1, keepdims=True)
    probs = raised / totals
    context = jnp.einsum(
        "hqk,khd->qhd",
        probs.astype(jnp.bfloat16),
        split_heads(value_rows),
        preferred_element_type=jnp.float32,
    )
    return (context.reshape(query_rows.shape).astype(jnp.bfloat16), largest + jnp.log(totals))


def attend_back(inputs):
    query_rows, key_rows, value_rows, visible, kept_lse, context_grad = inputs
    query_heads = split_heads(query_rows)
    key_heads = split_heads(key_rows)
    value_heads = split_heads(value_rows)
    grad_heads = split_heads(context_grad)
    probs = jnp.exp(masked_scores(query_heads, key_heads, visible) - kept_lse)
    prob_grad = jnp.einsum(
        "qhd,khd->hqk", grad_heads, value_heads, preferred_element_type=jnp.float32
    )
    centered = prob_grad - jnp.sum(prob_grad * probs, axis=-1, keepdims=True)
    score_grad = (probs * centered).astype(jnp.bfloat16)
    query_grad = (
        jnp.einsum("hqk,khd->qhd", score_grad, key_heads, preferred_element_type=jnp.float32)
        * scaling
    )
    key_grad = (
        jnp.einsum("hqk,qhd->khd", score_grad, query_heads, preferred_element_type=jnp.float32)
        * scaling
    )
    value_grad = jnp.einsum(
        "hqk,qhd->khd", probs.astype(jnp.bfloat16), grad_heads, preferred_element_type=jnp.float32
    )
    return (
        query_grad.reshape(query_rows.shape),
        key_grad.reshape(key_rows.shape),
        value_grad.reshape(value_rows.shape),
    )


class Links:
    def __init__(self, groups, owners):
        self.groups, self.owners = groups, owners
        self.A = 4 if owners % 4 == 0 else 1
        self.B = owners // self.A
        A, B = self.A, self.B
        self.ring_a = [(a * B + b, (a + 1) % A * B + b) for a in range(A) for b in range(B)]
        self.ring_b = [(a * B + b, a * B + (b + 1) % B) for a in range(A) for b in range(B)]

    def place(self):
        vocab = lax.axis_index("vocab")
        return vocab // self.B, vocab % self.B

    def step_a(self, piece):
        return lax.ppermute(piece, "vocab", self.ring_a)

    def step_b(self, piece):
        return lax.ppermute(piece, "vocab", self.ring_b)

    def swap(self, piece, bit):
        return lax.ppermute(piece, "dp", [(i, i ^ bit) for i in range(self.groups)])

    def spread(self, piece, axis=0):
        a, b = self.place()
        shape = piece.shape[:axis] + (self.owners,) + piece.shape[axis:]
        out = jnp.zeros(shape, piece.dtype)
        held = piece
        for k in range(self.A):
            if k:
                held = self.step_a(held)
            row = held
            for m in range(self.B):
                if m:
                    row = self.step_b(row)
                where = (a - k) % self.A * self.B + (b - m) % self.B
                out = lax.dynamic_update_index_in_dim(out, row, where, axis)
        return out

    def fold(self, total, axis=0):
        a, b = self.place()
        shape = total.shape[:axis] + (self.A, self.B) + total.shape[axis + 1 :]
        total = total.reshape(shape)

        def ring(whole, count, here, step, axis):
            def block(index):
                return lax.dynamic_index_in_dim(whole, index % count, axis, keepdims=False)

            held = block(here - 1 + count)
            for s in range(1, count):
                held = add(step(held), block(here - 1 - s + 2 * count))
            return held

        total = ring(total, self.B, b, self.step_b, axis + 1)
        return ring(total, self.A, a, self.step_a, axis)

    def far(self, piece, first):
        bit = first
        while bit < self.groups:
            piece = add(piece, self.swap(piece, bit))
            bit *= 2
        return piece


def add(left, right):
    return (left.astype(jnp.float32) + right.astype(jnp.float32)).astype(jnp.bfloat16)


def gelu(inner):
    return inner * (0.5 * (1.0 + lax.erf(inner * (1.0 / math.sqrt(2.0)))))


def put(blocks, where, axis):
    shape = blocks[0].shape[:axis] + (len(blocks),) + blocks[0].shape[axis:]
    out = jnp.zeros(shape, blocks[0].dtype)
    for block, index in zip(blocks, where):
        out = lax.dynamic_update_index_in_dim(out, block, index, axis)
    return out


def pick(stacked, index, axis=0):
    return lax.dynamic_index_in_dim(stacked, index, axis, keepdims=False)


def on_device(
    groups,
    owners,
    token_ids,
    lengths,
    word_table,
    position_table,
    embed_gain,
    embed_bias,
    query_weight,
    query_bias,
    key_weight,
    value_weight,
    value_bias,
    output_weight,
    output_bias,
    middle_gain,
    middle_bias,
    inner_weight,
    inner_bias,
    outer_weight,
    outer_bias,
    final_gain,
    final_bias,
    cotangent,
):
    links = Links(groups, owners)
    table_rows, width = word_table.shape
    full_len = token_ids.shape[1]
    piece_rows = query_weight.shape[0]
    hidden = inner_weight.shape[1]
    cap = 2 * full_len // owners
    dp = lax.axis_index("dp")
    core, quarter = dp % 2, dp % 4
    ids = token_ids.reshape(full_len)

    owner = ids // table_rows
    local = ids - owner * table_rows
    onehot = owner[:, None] == lax.iota(jnp.int32, owners)[None, :]
    before = lax.iota(jnp.int32, full_len)
    lower = (before[:, None] > before[None, :]).astype(jnp.bfloat16)
    ranks = matmul(lower, onehot.astype(jnp.bfloat16))
    rank = jnp.sum(jnp.where(onehot, ranks, 0.0), axis=1).astype(jnp.int32)
    slot = owner * cap + rank
    slots = lax.iota(jnp.int32, owners * cap)
    sent_ids = jnp.sum(
        jnp.where(slots[:, None] == slot[None, :], local[None, :] + 1, 0), axis=1
    ) - 1
    held_ids = lax.all_to_all(sent_ids.reshape(owners, cap), "vocab", 0, 0, tiled=True).reshape(-1)
    picked = jnp.take(word_table, jnp.maximum(held_ids, 0), axis=0)
    arrived = lax.all_to_all(picked.reshape(owners, cap, width), "vocab", 0, 0, tiled=True)
    route = (slot[:, None] == slots[None, :]).astype(jnp.bfloat16)
    embedded = matmul(route, arrived.reshape(owners * cap, width))

    vectors = [
        embed_gain, embed_bias, query_bias, value_bias, output_bias, middle_gain, middle_bias,
        outer_bias, final_gain, final_bias,
    ]
    small = jnp.concatenate(vectors + [inner_bias])
    small_rows = -(-small.shape[0] // width)
    small = jnp.pad(small, (0, small_rows * width - small.shape[0])).reshape(small_rows, width)
    place_part = position_table.shape[0] // 2
    place_half = lax.dynamic_slice_in_dim(position_table, core * place_part, place_part, 0)
    first_message = links.spread(jnp.concatenate([place_half, small]))
    place_here = first_message[:, :place_part]
    place_there = links.swap(place_here, 1)
    place_rows = put([place_here, place_there], [core, 1 - core], 1).reshape(full_len, width)
    small = first_message[:, place_part:].reshape(owners, small_rows * width)
    vector = [
        small[:, i * piece_rows : (i + 1) * piece_rows].reshape(width).astype(jnp.float32)
        for i in range(len(vectors))
    ]
    (
        embed_scale, embed_shift, query_shift, value_shift, output_shift, middle_scale,
        middle_shift, outer_shift, final_scale, final_shift,
    ) = vector
    inner_shift = (
        small[:, len(vectors) * piece_rows :][:, : inner_bias.shape[0]]
        .reshape(hidden)
        .astype(jnp.float32)
    )

    square = jnp.stack([query_weight, key_weight, value_weight, output_weight])
    pair_here = links.spread(lax.dynamic_slice_in_dim(square, 2 * core, 2, 0), 1)
    pair_there = links.swap(pair_here, 1)
    four = put([pair_here, pair_there], [core, 1 - core], 0).reshape(4, width, width)
    query_matrix, key_matrix, value_matrix, output_matrix = (four[i] for i in range(4))

    blocks = [quarter, quarter ^ 1, quarter ^ 2, quarter ^ 3]

    def quad(piece):
        beside = links.swap(piece, 1)
        beyond = links.swap(piece, 2)
        return [piece, beside, beyond, links.swap(beyond, 1)]

    inner_part = links.spread(lax.dynamic_slice_in_dim(inner_weight, quarter * width, width, 1))
    inner_matrix = put(quad(inner_part.reshape(width, width)), blocks, 0)
    outer_part = links.spread(
        lax.dynamic_slice_in_dim(outer_weight, quarter * piece_rows, piece_rows, 0)
    )
    outer_matrix = put(quad(outer_part), blocks, 1).reshape(hidden, width)

    summed = embedded + place_rows.astype(jnp.float32)
    normed, hat_embed, inv_embed = normalize(summed, embed_scale, embed_shift)
    normed_low = normed.astype(jnp.bfloat16)
    query_low = (matmul(normed_low, query_matrix) + query_shift).astype(jnp.bfloat16)
    key_low = matmul(normed_low, key_matrix).astype(jnp.bfloat16)
    value_low = (matmul(normed_low, value_matrix) + value_shift).astype(jnp.bfloat16)
    visible = lax.iota(jnp.int32, full_len) < lengths[0]
    context, lse_kept = attend((query_low, key_low, value_low, visible))
    attended = matmul(context, output_matrix) + output_shift
    middle, hat_middle, inv_middle = normalize(normed + attended, middle_scale, middle_shift)
    middle_low = middle.astype(jnp.bfloat16)
    inner = (
        jnp.concatenate([matmul(middle_low, inner_matrix[i]) for i in range(4)], axis=1)
        + inner_shift
    )
    activated = gelu(inner).astype(jnp.bfloat16)
    branch = matmul(activated, outer_matrix) + outer_shift
    result, hat_final, inv_final = normalize(middle + branch, final_scale, final_shift)
    output = result.astype(jnp.bfloat16).reshape(1, full_len, width)

    upstream = cotangent.reshape(full_len, width).astype(jnp.float32)
    final_gain_gradient = jnp.sum(upstream * hat_final, axis=0)
    final_bias_gradient = jnp.sum(upstream, axis=0)
    second = normalize_back(upstream, hat_final, inv_final, final_scale)
    branch_grad = second.astype(jnp.bfloat16)
    outer_bias_gradient = jnp.sum(branch_grad.astype(jnp.float32), axis=0)

    def shared(parts):
        beside = links.swap(jnp.stack([parts[1], parts[3]]), 1)
        near, across = add(parts[0], beside[0]), add(parts[2], beside[1])
        whole = add(near, links.swap(across, 2))
        return links.far(links.fold(whole), 4)

    outer_grad = contract_rows(activated, branch_grad).astype(jnp.bfloat16)
    outer_grad = outer_grad.reshape(owners, 4, piece_rows, width)
    outer_share = shared([pick(outer_grad, i, 1) for i in blocks])
    inner_grad = (times_transposed(branch_grad, outer_matrix) * gelu_slope(inner)).astype(
        jnp.bfloat16
    )
    inner_bias_gradient = jnp.sum(inner_grad.astype(jnp.float32), axis=0)
    inner_parts = [inner_grad[:, i * width : (i + 1) * width] for i in range(4)]
    inner_grads = jnp.stack(
        [contract_rows(middle_low, part).astype(jnp.bfloat16) for part in inner_parts]
    ).reshape(4, owners, piece_rows, width)
    inner_share = shared([pick(inner_grads, i) for i in blocks])
    middle_grad = second + sum(
        times_transposed(inner_parts[i], inner_matrix[i]) for i in range(4)
    )
    middle_gain_gradient = jnp.sum(middle_grad * hat_middle, axis=0)
    middle_bias_gradient = jnp.sum(middle_grad, axis=0)
    first = normalize_back(middle_grad, hat_middle, inv_middle, middle_scale)
    attended_grad = first.astype(jnp.bfloat16)
    output_bias_gradient = jnp.sum(attended_grad.astype(jnp.float32), axis=0)
    output_grad = contract_rows(context, attended_grad).astype(jnp.bfloat16)
    context_grad = times_transposed(attended_grad, output_matrix).astype(jnp.bfloat16)
    query_grad, key_grad, value_grad = attend_back(
        (query_low, key_low, value_low, visible, lse_kept, context_grad)
    )
    query_low_grad = query_grad.astype(jnp.bfloat16)
    key_low_grad = key_grad.astype(jnp.bfloat16)
    value_low_grad = value_grad.astype(jnp.bfloat16)
    query_bias_gradient = jnp.sum(query_low_grad.astype(jnp.float32), axis=0)
    value_bias_gradient = jnp.sum(value_low_grad.astype(jnp.float32), axis=0)
    normed_grad = (
        first
        + times_transposed(query_low_grad, query_matrix)
        + times_transposed(key_low_grad, key_matrix)
        + times_transposed(value_low_grad, value_matrix)
    )
    embed_gain_gradient = jnp.sum(normed_grad * hat_embed, axis=0)
    embed_bias_gradient = jnp.sum(normed_grad, axis=0)
    summed_grad = normalize_back(normed_grad, hat_embed, inv_embed, embed_scale)
    embedded_grad = summed_grad.astype(jnp.bfloat16)

    leaving = jnp.einsum(
        "ts,td->sd", route, embedded_grad, preferred_element_type=jnp.float32
    ).astype(jnp.bfloat16)
    landed = lax.all_to_all(leaving.reshape(owners, cap, width), "vocab", 0, 0, tiled=True)
    landed = landed.reshape(1, owners * cap, width)
    known = held_ids[None]
    bit = 1
    while bit < groups:
        low_side = (dp // bit) % 2 == 0

        def joined(own, bit=bit, low_side=low_side):
            other = links.swap(own, bit)
            return jnp.concatenate(
                [jnp.where(low_side, own, other), jnp.where(low_side, other, own)]
            )

        landed, known = joined(landed), joined(known)
        bit *= 2
    landed, known = landed.reshape(-1, width), known.reshape(-1)
    half_rows = table_rows // 2
    half_ids = core * half_rows + lax.iota(jnp.int32, half_rows)
    table_half = matmul(
        (half_ids[:, None] == known[None, :]).astype(jnp.bfloat16), landed
    ).astype(jnp.bfloat16)
    table_other = links.swap(table_half, 1)
    table_gradient = jnp.concatenate(
        [
            jnp.where(core == 0, table_half, table_other).astype(jnp.float32),
            jnp.where(core == 0, table_other, table_half).astype(jnp.float32),
        ]
    )

    square_grads = jnp.stack(
        [
            contract_rows(normed_low, query_low_grad).astype(jnp.bfloat16),
            contract_rows(normed_low, key_low_grad).astype(jnp.bfloat16),
            contract_rows(normed_low, value_low_grad).astype(jnp.bfloat16),
            output_grad,
        ]
    ).reshape(2, 2, owners, piece_rows, width)
    mine = add(pick(square_grads, core), links.swap(pick(square_grads, 1 - core), 1))
    pair_share = links.far(links.fold(mine, 1), 2)
    pair_other = links.swap(pair_share, 1)
    four_shares = put([pair_share, pair_other], [core, 1 - core], 0)
    four_shares = four_shares.reshape(4, piece_rows, width).astype(jnp.float32)

    place_grads = summed_grad.astype(jnp.bfloat16).reshape(owners, 2, place_part, width)
    place_mine = add(
        pick(place_grads, core, 1), links.swap(pick(place_grads, 1 - core, 1), 1)
    )
    place_share = links.far(links.fold(place_mine), 2)
    place_other = links.swap(place_share, 1)
    position_gradient = put([place_share, place_other], [core, 1 - core], 0)
    position_gradient = position_gradient.reshape(2 * place_part, width).astype(jnp.float32)

    def regroup(share, axis):
        return put(quad(share), blocks, axis).astype(jnp.float32)

    inner_weight_gradient = regroup(inner_share, 1).reshape(piece_rows, hidden)
    outer_weight_gradient = regroup(outer_share, 0).reshape(4 * piece_rows, width)

    sums = [
        embed_gain_gradient, embed_bias_gradient, query_bias_gradient, value_bias_gradient,
        output_bias_gradient, middle_gain_gradient, middle_bias_gradient, outer_bias_gradient,
        final_gain_gradient, final_bias_gradient,
    ]
    table = jnp.concatenate(
        [item.reshape(owners, piece_rows) for item in sums]
        + [inner_bias_gradient.reshape(owners, inner_bias.shape[0])],
        axis=1,
    ).astype(jnp.bfloat16)
    vector_share = links.far(links.fold(table), 1).astype(jnp.float32)
    pieces = [vector_share[i * piece_rows : (i + 1) * piece_rows] for i in range(len(sums))]
    inner_bias_gradient = vector_share[len(sums) * piece_rows :]
    (
        embed_gain_gradient, embed_bias_gradient, query_bias_gradient, value_bias_gradient,
        output_bias_gradient, middle_gain_gradient, middle_bias_gradient, outer_bias_gradient,
        final_gain_gradient, final_bias_gradient,
    ) = pieces
    return (
        output,
        table_gradient,
        position_gradient,
        embed_gain_gradient,
        embed_bias_gradient,
        four_shares[0],
        query_bias_gradient,
        four_shares[1],
        four_shares[2],
        value_bias_gradient,
        four_shares[3],
        output_bias_gradient,
        middle_gain_gradient,
        middle_bias_gradient,
        inner_weight_gradient,
        inner_bias_gradient,
        outer_weight_gradient,
        outer_bias_gradient,
        final_gain_gradient,
        final_bias_gradient,
    )


def solution(mesh):
    return jax.shard_map(
        functools.partial(on_device, mesh.shape["dp"], mesh.shape["vocab"]),
        mesh=mesh,
        in_specs=(
            P(("dp", "vocab"), None),
            P(("dp", "vocab")),
            P("vocab", None),
            P("vocab", None),
            P("vocab"),
            P("vocab"),
            P("vocab", None),
            P("vocab"),
            P("vocab", None),
            P("vocab", None),
            P("vocab"),
            P("vocab", None),
            P("vocab"),
            P("vocab"),
            P("vocab"),
            P("vocab", None),
            P("vocab"),
            P("vocab", None),
            P("vocab"),
            P("vocab"),
            P("vocab"),
            P(("dp", "vocab"), None, None),
        ),
        out_specs=(
            P(("dp", "vocab"), None, None),
            P("vocab", None),
            P("vocab", None),
            P("vocab"),
            P("vocab"),
            P("vocab", None),
            P("vocab"),
            P("vocab", None),
            P("vocab", None),
            P("vocab"),
            P("vocab", None),
            P("vocab"),
            P("vocab"),
            P("vocab"),
            P("vocab", None),
            P("vocab"),
            P("vocab", None),
            P("vocab"),
            P("vocab"),
            P("vocab"),
        ),
        check_vma=False,
    )
```

time: 1380 us -> 627 us (0.45)
  waiting for transfers between devices: 919 us -> 225 us
  blocking collectives: 169 us -> 0 us
  starting transfers between devices: 0.85 us -> 89 us
  local copies, waits for them, and re-layouts: 42.7 us -> 119 us
  matrix products: 172 us -> 124 us
  between operations: 17.6 us -> 3.25 us
    reduce_scatter x8 -> x0, waiting for transfers between devices: 472 us -> none  [the longest x1 98.8 us: on_device(): lax.psum_scatter(outer_weight_gradient.astype(jnp.bfloat16), 'vocab', sca...]
    all_gather x7 -> x0, waiting for transfers between devices: 349 us -> none  [the longest x1 77.1 us: on_device(): lax.all_gather(inner_weight, 'vocab', axis=0, tiled=True)]
    ppermute x0 -> x79, waiting for transfers between devices: none -> 225 us  [the longest x31 87.5 us: swap(): return lax.ppermute(piece, 'dp', [(i, i ^ bit) for i in range(self.groups)])]
    psum x1 -> x0, waiting for transfers between devices: 92.9 us -> none  [on_device(): lax.psum(running.astype(jnp.bfloat16), 'dp').astype(jnp.float32)]
    all_gather x3 -> x0, blocking collectives: 88.6 us -> none  [the longest x1 33.9 us: on_device(): lax.all_gather(position_table, 'vocab', axis=0, tiled=True)]
    unnamed x2 -> x0, blocking collectives: 73.3 us -> none
    ppermute x0 -> x79, starting transfers between devices: none -> 72.6 us  [the longest x27 33.9 us: step_a(): return lax.ppermute(piece, 'vocab', self.ring_a)]
    dot_general x8 -> x1, matrix products: 72.3 us -> 2.29 us  [on_device(): jnp.einsum('ts,td->sd', route, embedded_grad, preferred_element_type=jnp....]
  transfers between devices with their start and end apart: 16 -> 82, of which waited for: 15 -> 27; matrix products, arithmetic and copies ran while one was open for 12% -> 24% of each run, Pallas kernels for 0% -> 0%
where the time goes in v1:
time: 627 us; the launch traced here: 618 us
  waiting for transfers between devices  225 us (36%)
  matrix products  124 us (20%)
  local copies, waits for them, and re-layouts  119 us (19%)
  starting transfers between devices  89 us (14%)
  other arithmetic  57.6 us (9%)
    ppermute x31, waiting for transfers between devices, swap(): return lax.ppermute(piece, 'dp', [(i, i ^ bit) for i in range(self.groups)])  87.5 us
    ppermute x27, waiting for transfers between devices, step_a(): return lax.ppermute(piece, 'vocab', self.ring_a)  70.6 us
    ppermute x21, waiting for transfers between devices, step_b(): return lax.ppermute(piece, 'vocab', self.ring_b)  67.2 us
    dynamic_update_slice x21, local copies, waits for them, and re-layouts, put(): out = lax.dynamic_update_index_in_dim(out, block, index, axis)  41.2 us
    dot_general x12, matrix products, matmul(): return jnp.dot(left, right, preferred_element_type=jnp.float32)  40.1 us
    ppermute x27, starting transfers between devices, step_a(): return lax.ppermute(piece, 'vocab', self.ring_a)  33.9 us
    dot_general x9, matrix products, times_transposed(): jnp.einsum('tj,ij->ti', left, right, preferred_element_type=jnp.float32)  32.7 us
    ppermute x21, starting transfers between devices, step_b(): return lax.ppermute(piece, 'vocab', self.ring_b)  26.7 us
  transfers between devices with their start and end apart: 82, of which 27 were waited for; matrix products, arithmetic and copies ran while one was open for 24% of the time, Pallas kernels for 0%

profile of v1, /device:TPU:0, one launch (start us, length us, event | category | flops | bytes accessed | tf_op | source)
XLA Modules:
  0.0 618.1 jit_solution(13371377404015219230)
XLA Ops:
  0.7 7.5 %concatenate.55 = bf16[1344]{0:T(1024)(128)(2,1)S(1)} concatenate(bf16[96]{0:T(256)(128)(2,1)} %param.26, bf16[96]{0:T(256)(128)(2,1)} %param.27, bf16[96]{0:T(256)(128)(2,1)} %param.29, bf16[96]{0:T(256)(128)(2,1)} %param.32, bf16[96]{0:T(256)(128)(2,1)} %param.34, bf16[96]{0:T(256)(128)(2,1)} %param.35, bf16[96]{0:T(256)(128)(2,1)} %param.36, bf16[96]{0:T(256)(128)(2,1)} %param.40, ...), dimensions={0} | concatenate | bytes 5376 | tf_op jit(solution)/shard_map/concatenate | solution.py:250
  31.7 7.9 %gather_fusion = bf16[1024,768]{1,0:T(8,128)(2,1)S(1)} fusion(bf16[3840,768]{1,0:T(8,128)(2,1)} %param.24, s32[1024]{0:T(1024)S(1)} %bitcast_clamp_fusion), kind=kCustom, calls=%fused_computation | custom fusion | bytes 3149824 | tf_op jit(solution)/shard_map/jit(_take)/gather | solution.py:241
  42.7 6.1 all-to-all-start.1
  53.5 14.0 %collective-permute-done.2 = bf16[34,768]{1,0:T(8,128)(2,1)S(1)} collective-permute-done((bf16[34,768]{1,0:T(8,128)(2,1)S(1)}, bf16[34,768]{1,0:T(8,128)(2,1)S(1)}, u32[]{:S(2)}, u32[]{:S(2)}) %collective-permute-start.2) | collective-permute-done | bytes 52256 | tf_op jit(solution)/shard_map/ppermute | solution.py:126
  68.2 15.1 %collective-permute-done.3 = bf16[34,768]{1,0:T(8,128)(2,1)S(1)} collective-permute-done((bf16[34,768]{1,0:T(8,128)(2,1)S(1)}, bf16[34,768]{1,0:T(8,128)(2,1)S(1)}, u32[]{:S(2)}, u32[]{:S(2)}) %collective-permute-start.3) | collective-permute-done | bytes 52256 | tf_op jit(solution)/shard_map/ppermute | solution.py:123
  84.8 6.1 collective-permute-start.9
  132.0 8.5 %collective-permute-done.32 = bf16[96,768]{1,0:T(8,128)(2,1)S(1)} collective-permute-done((bf16[96,768]{1,0:T(8,128)(2,1)S(1)}, bf16[96,768]{1,0:T(8,128)(2,1)S(1)}, u32[]{:S(2)}, u32[]{:S(2)}) %collective-permute-start.32) | collective-permute-done | bytes 147488 | tf_op jit(solution)/shard_map/ppermute | solution.py:126
  159.0 6.9 %collective-permute-done.14 = bf16[2,96,768]{2,1,0:T(8,128)(2,1)S(1)} collective-permute-done((bf16[2,96,768]{2,1,0:T(8,128)(2,1)S(1)}, bf16[2,96,768]{2,1,0:T(8,128)(2,1)S(1)}, u32[]{:S(2)}, u32[]{:S(2)}) %collective-permute-start.14) | collective-permute-done | bytes 294944 | tf_op jit(solution)/shard_map/ppermute | solution.py:126
  173.1 17.9 %collective-permute-done.24 = bf16[768,768]{1,0:T(8,128)(2,1)} collective-permute-done((bf16[768,768]{1,0:T(8,128)(2,1)}, bf16[768,768]{1,0:T(8,128)(2,1)}, u32[]{:S(2)}, u32[]{:S(2)}) %collective-permute-start.24) | collective-permute-done | bytes 1179680 | tf_op jit(solution)/shard_map/ppermute | solution.py:129
  252.9 9.1 %fusion.111 = (bf16[3072]{0:T(1024)(128)(2,1)S(1)}, bf16[512,3072]{1,0:T(8,128)(2,1)}) fusion(f32[3072]{0:T(1024)S(1)} %copy-done.37, f32[512,768]{1,0:T(8,128)S(1)} %fusion.59, f32[512,768]{1,0:T(8,128)S(1)} %fusion.58, f32[512,768]{1,0:T(8,128)S(1)} %fusion.56, f32[512,768]{1,0:T(8,128)S(1)} %fusion.54, bf16[3072,768]{1,0:T(8,128)(2,1)} %bitcast.85, ...), kind=kOutput, calls=%fused_computation.355 | convolution fusion | flops 2439902208 | bytes 15747072 | tf_op jit(solution)/shard_map/tj,ij->ti/dot_general | solution.py:47
  292.4 7.9 %bitcast_reduce_fusion = (bf16[12,64]{1,0:T(8,128)(2,1)S(1)}, bf16[12,64,512]{2,1,0:T(8,128)(2,1)}) fusion(bf16[512,12,64]{0,2,1:T(8,128)(2,1)} %bitcast.444, f32[12,512,512]{1,2,0:T(8,128)} %copy-done.2, f32[12,512]{1,0:T(8,128)S(1)} %log_add_fusion), kind=kOutput, calls=%fused_computation.162 | convolution fusion | flops 409730304 | bytes 14181888 | tf_op jit(solution)/shard_map/hqk,qhd->khd/dot_general | solution.py:99
  300.4 9.1 %multiply_reduce_fusion = (f32[12,512]{1,0:T(8,128)S(1)}, f32[12,512,512]{1,2,0:T(8,128)}) fusion(f32[12,512,512]{1,2,0:T(8,128)} %copy-done.2, f32[12,512]{1,0:T(8,128)S(1)} %log_add_fusion, bf16[512,12,64]{0,2,1:T(8,128)(2,1)S(1)} %bitcast.445, bf16[512,12,64]{0,2,1:T(8,128)(2,1)S(1)} %bitcast.462), kind=kOutput, calls=%fused_computation.6 | convolution fusion | flops 412084224 | bytes 26787840 | tf_op jit(solution)/shard_map/qhd,khd->hqk/dot_general | solution.py:86
  309.5 6.9 %multiply_convert_fusion = bf16[12,512,512]{1,2,0:T(8,128)(2,1)S(1)} fusion(f32[12,512,512]{1,2,0:T(8,128)} %get-tuple-element.107, f32[12,512,512]{1,2,0:T(8,128)S(1)} %bitcast.436, f32[12,512]{1,0:T(8,128)S(1)} %get-tuple-element.106, f32[12,512]{1,0:T(8,128)S(1)} %log_add_fusion), kind=kLoop, calls=%fused_computation.5 | loop fusion | flops 12582912 | bytes 31506432 | tf_op jit(solution)/shard_map/convert_element_type | solution.py:90
  369.9 21.1 %collective-permute-done.49 = bf16[1344]{0:T(1024)(128)(2,1)S(1)} collective-permute-done((bf16[1344]{0:T(1024)(128)(2,1)S(1)}, bf16[1344]{0:T(1024)(128)(2,1)S(1)}, u32[]{:S(2)}, u32[]{:S(2)}) %collective-permute-start.49) | collective-permute-done | bytes 2720 | tf_op jit(solution)/shard_map/ppermute | solution.py:123
  391.0 6.9 %collective-permute-start.50 = (bf16[1344]{0:T(1024)(128)(2,1)S(1)}, bf16[1344]{0:T(1024)(128)(2,1)S(1)}, u32[]{:S(2)}, u32[]{:S(2)}) collective-permute-start(bf16[1344]{0:T(1024)(128)(2,1)S(1)} %add_convert_fusion.12), channel_id=1, source_target_pairs={{0,2},{1,3},{2,4},{3,5},{4,6},{5,7},{6,0},{7,1},{8,10},{9,11},{10,... | collective-permute-start | bytes 8072 | tf_op jit(solution)/shard_map/ppermute | solution.py:123
  433.3 20.1 %collective-permute-done.55 = bf16[2,4,96,768]{3,2,0,1:T(8,128)(2,1)S(1)} collective-permute-done((bf16[2,4,96,768]{3,2,0,1:T(8,128)(2,1)S(1)}, bf16[2,4,96,768]{3,2,0,1:T(8,128)(2,1)S(1)}, u32[]{:S(2)}, u32[]{:S(2)}) %collective-permute-start.55) | collective-permute-done | bytes 1179680 | tf_op jit(solution)/shard_map/ppermute | solution.py:126
  463.9 18.7 %collective-permute-done.71 = bf16[8,96,768]{2,1,0:T(8,128)(2,1)S(1)} collective-permute-done((bf16[8,96,768]{2,1,0:T(8,128)(2,1)S(1)}, bf16[8,96,768]{2,1,0:T(8,128)(2,1)S(1)}, u32[]{:S(2)}, u32[]{:S(2)}) %collective-permute-start.71) | collective-permute-done | bytes 1179680 | tf_op jit(solution)/shard_map/ppermute | solution.py:129
  486.3 11.3 %collective-permute-done.72 = bf16[4,96,768]{2,1,0:T(8,128)(2,1)S(1)} collective-permute-done((bf16[4,96,768]{2,1,0:T(8,128)(2,1)S(1)}, bf16[4,96,768]{2,1,0:T(8,128)(2,1)S(1)}, u32[]{:S(2)}, u32[]{:S(2)}) %collective-permute-start.72) | collective-permute-done | bytes 589856 | tf_op jit(solution)/shard_map/ppermute | solution.py:126
  498.6 6.2 collective-permute-done.73
  506.4 43.7 %collective-permute-done.39 = bf16[2,1024,768]{2,1,0:T(8,128)(2,1)S(1)} collective-permute-done((bf16[2,1024,768]{2,1,0:T(8,128)(2,1)S(1)}, bf16[2,1024,768]{2,1,0:T(8,128)(2,1)S(1)}, u32[]{:S(2)}, u32[]{:S(2)}) %collective-permute-start.39) | collective-permute-done | bytes 3145760 | tf_op jit(solution)/shard_map/ppermute | solution.py:129
  551.3 14.1 %fusion.17 = bf16[1920,768]{1,0:T(8,128)(2,1)} fusion(bf16[4096,768]{1,0:T(8,128)(2,1)S(1)} %bitcast.448, s32[4096]{0:T(1024)S(1)} %bitcast.495, s32[1920]{0:T(1024)S(1)} %copy-done.44), kind=kOutput, calls=%fused_computation.33 | convolution fusion | flops 12088934400 | bytes 9264640 | tf_op jit(solution)/shard_map/dot_general | solution.py:39
  567.4 7.5 %collective-permute-done.66 = bf16[96,768]{1,0:T(8,128)(2,1)S(1)} collective-permute-done((bf16[96,768]{1,0:T(8,128)(2,1)S(1)}, bf16[96,768]{1,0:T(8,128)(2,1)S(1)}, u32[]{:S(2)}, u32[]{:S(2)}) %collective-permute-start.66) | collective-permute-done | bytes 147488 | tf_op jit(solution)/shard_map/ppermute | solution.py:123
  584.8 6.2 %dynamic_update_slice.229 = bf16[96,4,768]{2,1,0:T(4,128)(2,1)} dynamic-update-slice(bf16[96,4,768]{2,1,0:T(4,128)(2,1)} %copy.190, bf16[96,1,768]{2,1,0:T(2,128)(2,1)S(1)} %copy.191, s32[]{:T(128)} %constant.642.clone.1, s32[]{:T(128)S(6)} %select_n.566, s32[]{:T(128)} %constant.642.clone.1) | dynamic-update-slice | bytes 294916 | tf_op jit(solution)/shard_map/jit(dynamic_update_index_in_dim)/dynamic_update_slice | solution.py:184
  595.6 6.2 %dynamic_update_slice.230 = bf16[96,4,768]{2,1,0:T(4,128)(2,1)} dynamic-update-slice(bf16[96,4,768]{2,1,0:T(4,128)(2,1)} %dynamic_update_slice.229, bf16[96,1,768]{2,1,0:T(2,128)(2,1)S(1)} %copy.192, s32[]{:T(128)} %constant.642.clone.1, s32[]{:T(128)S(6)} %select_n.567, s32[]{:T(128)} %constant.642.clone.1) | dynamic-update-slice | bytes 294916 | tf_op jit(solution)/shard_map/jit(dynamic_update_index_in_dim)/dynamic_update_slice | solution.py:184
  (506 shorter events, 329.8 us)
Async XLA Ops:
  8.3 43.2 %collective-permute-start = (bf16[34,768]{1,0:T(8,128)(2,1)S(1)}, bf16[34,768]{1,0:T(8,128)(2,1)S(1)}, u32[]{:S(2)}, u32[]{:S(2)}) collective-permute-start(bf16[34,768]{1,0:T(8,128)(2,1)S(1)} %pad_maximum_fusion.6), channel_id=1, source_target_pairs={{0,1},{1,0},{2,3},{3,2},{4,5},{5,4},{6,7},{7,6},{8,9},{9,8},{10,11... | collective-permute-start | bytes 156680 | tf_op jit(solution)/shard_map/ppermute | solution.py:126
  11.3 41.6 %collective-permute-start.1 = (bf16[34,768]{1,0:T(8,128)(2,1)S(1)}, bf16[34,768]{1,0:T(8,128)(2,1)S(1)}, u32[]{:S(2)}, u32[]{:S(2)}) collective-permute-start(bf16[34,768]{1,0:T(8,128)(2,1)S(1)} %pad_maximum_fusion.6), channel_id=1, source_target_pairs={{0,2},{1,3},{2,4},{3,5},{4,6},{5,7},{6,0},{7,1},{8,10},{9,11},{10,... | collective-permute-start | bytes 156680 | tf_op jit(solution)/shard_map/ppermute | solution.py:123
  15.6 69.1 %collective-permute-start.16 = (bf16[96,768]{1,0:T(8,128)(2,1)}, bf16[96,768]{1,0:T(8,128)(2,1)}, u32[]{:S(2)}, u32[]{:S(2)}) collective-permute-start(bf16[96,768]{1,0:T(8,128)(2,1)} %get-tuple-element.49), channel_id=1, source_target_pairs={{0,1},{1,0},{2,3},{3,2},{4,5},{5,4},{6,7},{7,6},{8,9},{9,8},{10,11... | collective-permute-start | bytes 442376 | tf_op jit(solution)/shard_map/ppermute | solution.py:126
  16.1 76.3 %collective-permute-start.17 = (bf16[96,768]{1,0:T(8,128)(2,1)}, bf16[96,768]{1,0:T(8,128)(2,1)}, u32[]{:S(2)}, u32[]{:S(2)}) collective-permute-start(bf16[96,768]{1,0:T(8,128)(2,1)} %get-tuple-element.49), channel_id=1, source_target_pairs={{0,2},{1,3},{2,4},{3,5},{4,6},{5,7},{6,0},{7,1},{8,10},{9,11},{10,... | collective-permute-start | bytes 442376 | tf_op jit(solution)/shard_map/ppermute | solution.py:123
  42.7 155.3 %all-to-all-start.1 = ((bf16[8,128,768]{2,1,0:T(8,128)(2,1)}), bf16[8,128,768]{2,1,0:T(8,128)(2,1)}, u32[]{:S(2)}, u32[]{:S(2)}) async-start(bf16[8,128,768]{2,1,0:T(8,128)(2,1)} %broadcast_select_fusion.6), calls=%async_computation.1 | async-start | bytes 3145728 | tf_op jit(solution)/shard_map/all_to_all | solution.py:242
  48.8 47.7 %collective-permute-start.26 = (bf16[96,768]{1,0:T(8,128)(2,1)}, bf16[96,768]{1,0:T(8,128)(2,1)S(1)}, u32[]{:S(2)}, u32[]{:S(2)}) collective-permute-start(bf16[96,768]{1,0:T(8,128)(2,1)} %get-tuple-element.47), channel_id=1, source_target_pairs={{0,1},{1,0},{2,3},{3,2},{4,5},{5,4},{6,7},{7,6},{8,9},{9,8},{10,11... | collective-permute-start | bytes 442376 | tf_op jit(solution)/shard_map/ppermute | solution.py:126
  51.5 46.4 %collective-permute-start.27 = (bf16[96,768]{1,0:T(8,128)(2,1)}, bf16[96,768]{1,0:T(8,128)(2,1)S(1)}, u32[]{:S(2)}, u32[]{:S(2)}) collective-permute-start(bf16[96,768]{1,0:T(8,128)(2,1)} %get-tuple-element.47), channel_id=1, source_target_pairs={{0,2},{1,3},{2,4},{3,5},{4,6},{5,7},{6,0},{7,1},{8,10},{9,11},{10,... | collective-permute-start | bytes 442376 | tf_op jit(solution)/shard_map/ppermute | solution.py:123
  83.3 38.3 %collective-permute-start.8 = (bf16[2,96,768]{2,1,0:T(8,128)(2,1)}, bf16[2,96,768]{2,1,0:T(8,128)(2,1)S(1)}, u32[]{:S(2)}, u32[]{:S(2)}) collective-permute-start(bf16[2,96,768]{2,1,0:T(8,128)(2,1)} %get-tuple-element.51), channel_id=1, source_target_pairs={{0,1},{1,0},{2,3},{3,2},{4,5},{5,4},{6,7},{7,6},{8,9},{9,8},{10,11... | collective-permute-start | bytes 884744 | tf_op jit(solution)/shard_map/ppermute | solution.py:126
  84.8 37.6 %collective-permute-start.9 = (bf16[2,96,768]{2,1,0:T(8,128)(2,1)}, bf16[2,96,768]{2,1,0:T(8,128)(2,1)S(1)}, u32[]{:S(2)}, u32[]{:S(2)}) collective-permute-start(bf16[2,96,768]{2,1,0:T(8,128)(2,1)} %get-tuple-element.51), channel_id=1, source_target_pairs={{0,2},{1,3},{2,4},{3,5},{4,6},{5,7},{6,0},{7,1},{8,10},{9,11},{10,... | collective-permute-start | bytes 884744 | tf_op jit(solution)/shard_map/ppermute | solution.py:123
  115.5 38.1 %collective-permute-start.7 = (bf16[8,32,768]{2,1,0:T(8,128)(2,1)}, bf16[8,32,768]{2,1,0:T(8,128)(2,1)S(1)}, u32[]{:S(2)}, u32[]{:S(2)}) collective-permute-start(bf16[8,32,768]{2,1,0:T(8,128)(2,1)} %slice.184), channel_id=1, source_target_pairs={{0,8},{8,0},{16,24},{24,16},{1,9},{9,1},{17,25},{25,17},{2,10},{10... | collective-permute-start | bytes 1179656 | tf_op jit(solution)/shard_map/ppermute | solution.py:129
  145.0 46.1 %collective-permute-start.33 = (bf16[8,96,768]{2,1,0:T(8,128)(2,1)S(1)}, bf16[8,96,768]{2,1,0:T(8,128)(2,1)S(1)}, u32[]{:S(2)}, u32[]{:S(2)}) collective-permute-start(bf16[8,96,768]{2,1,0:T(8,128)(2,1)S(1)} %bitcast_dynamic-update-slice_fusion.28), channel_id=1, source_target_pairs={{0,8},{8,0},{16,24},{24,16},{1,9},{9,1},{17,25},{25,17},{2,10},{10... | collective-permute-start | bytes 3538952 | tf_op jit(solution)/shard_map/ppermute | solution.py:129
  153.6 37.5 %collective-permute-start.24 = (bf16[768,768]{1,0:T(8,128)(2,1)}, bf16[768,768]{1,0:T(8,128)(2,1)}, u32[]{:S(2)}, u32[]{:S(2)}) collective-permute-start(bf16[768,768]{1,0:T(8,128)(2,1)} %bitcast.62), channel_id=1, source_target_pairs={{0,16},{8,24},{16,0},{24,8},{1,17},{9,25},{17,1},{25,9},{2,18},{10... | collective-permute-start | bytes 3538952 | tf_op jit(solution)/shard_map/ppermute | solution.py:129
  156.5 38.0 %collective-permute-start.23 = (bf16[768,768]{1,0:T(8,128)(2,1)}, bf16[768,768]{1,0:T(8,128)(2,1)S(1)}, u32[]{:S(2)}, u32[]{:S(2)}) collective-permute-start(bf16[768,768]{1,0:T(8,128)(2,1)} %bitcast.62), channel_id=1, source_target_pairs={{0,8},{8,0},{16,24},{24,16},{1,9},{9,1},{17,25},{25,17},{2,10},{10... | collective-permute-start | bytes 3538952 | tf_op jit(solution)/shard_map/ppermute | solution.py:129
  166.6 39.7 %collective-permute-start.15 = (bf16[2,8,96,768]{3,2,1,0:T(8,128)(2,1)}, bf16[2,8,96,768]{3,2,1,0:T(8,128)(2,1)}, u32[]{:S(2)}, u32[]{:S(2)}) collective-permute-start(bf16[2,8,96,768]{3,2,1,0:T(8,128)(2,1)} %bitcast_dynamic-update-slice_fusion.20), channel_id=1, source_target_pairs={{0,8},{8,0},{16,24},{24,16},{1,9},{9,1},{17,25},{25,17},{2,10},{10... | collective-permute-start | bytes 7077896 | tf_op jit(solution)/shard_map/ppermute | solution.py:129
  341.3 85.6 %collective-permute-start.61 = (bf16[2,8,96,768]{3,2,1,0:T(8,128)(2,1)}, bf16[2,8,96,768]{3,2,1,0:T(8,128)(2,1)}, u32[]{:S(2)}, u32[]{:S(2)}) collective-permute-start(bf16[2,8,96,768]{3,2,1,0:T(8,128)(2,1)} %pad_maximum_fusion.4), channel_id=1, source_target_pairs={{0,8},{8,0},{16,24},{24,16},{1,9},{9,1},{17,25},{25,17},{2,10},{10... | collective-permute-start | bytes 7077896 | tf_op jit(solution)/shard_map/ppermute | solution.py:129
  343.5 85.6 %collective-permute-start.70 = (bf16[2,8,96,768]{3,2,1,0:T(8,128)(2,1)}, bf16[2,8,96,768]{3,2,1,0:T(8,128)(2,1)}, u32[]{:S(2)}, u32[]{:S(2)}) collective-permute-start(bf16[2,8,96,768]{3,2,1,0:T(8,128)(2,1)} %pad_maximum_fusion.5), channel_id=1, source_target_pairs={{0,8},{8,0},{16,24},{24,16},{1,9},{9,1},{17,25},{25,17},{2,10},{10... | collective-permute-start | bytes 7077896 | tf_op jit(solution)/shard_map/ppermute | solution.py:129
  355.1 65.1 %all-to-all-start.2 = ((bf16[8,128,768]{2,1,0:T(8,128)(2,1)}), bf16[8,128,768]{2,1,0:T(8,128)(2,1)S(1)}, u32[]{:S(2)}, u32[]{:S(2)}) async-start(bf16[8,128,768]{2,1,0:T(8,128)(2,1)} %bitcast.470), calls=%async_computation.2 | async-start | bytes 3145728 | tf_op jit(solution)/shard_map/all_to_all | solution.py:371
  366.0 55.9 %collective-permute-start.54 = (bf16[2,8,96,768]{3,2,1,0:T(8,128)(2,1)}, bf16[2,8,96,768]{3,2,1,0:T(8,128)(2,1)}, u32[]{:S(2)}, u32[]{:S(2)}) collective-permute-start(bf16[2,8,96,768]{3,2,1,0:T(8,128)(2,1)} %dynamic-slice_bitcast_fusion), channel_id=1, source_target_pairs={{0,8},{8,0},{16,24},{24,16},{1,9},{9,1},{17,25},{25,17},{2,10},{10... | collective-permute-start | bytes 7077896 | tf_op jit(solution)/shard_map/ppermute | solution.py:129
  430.7 52.0 %collective-permute-start.71 = (bf16[8,96,768]{2,1,0:T(8,128)(2,1)S(1)}, bf16[8,96,768]{2,1,0:T(8,128)(2,1)S(1)}, u32[]{:S(2)}, u32[]{:S(2)}) collective-permute-start(bf16[8,96,768]{2,1,0:T(8,128)(2,1)S(1)} %fusion.20), channel_id=1, source_target_pairs={{0,16},{8,24},{16,0},{24,8},{1,17},{9,25},{17,1},{25,9},{2,18},{10... | collective-permute-start | bytes 3538952 | tf_op jit(solution)/shard_map/ppermute | solution.py:129
  432.7 117.3 %collective-permute-start.39 = (bf16[2,1024,768]{2,1,0:T(8,128)(2,1)S(1)}, bf16[2,1024,768]{2,1,0:T(8,128)(2,1)S(1)}, u32[]{:S(2)}, u32[]{:S(2)}) collective-permute-start(bf16[2,1024,768]{2,1,0:T(8,128)(2,1)S(1)} %pad_maximum_fusion.3), channel_id=1, source_target_pairs={{0,16},{8,24},{16,0},{24,8},{1,17},{9,25},{17,1},{25,9},{2,18},{10... | collective-permute-start | bytes 9437192 | tf_op jit(solution)/shard_map/ppermute | solution.py:129
  498.6 66.8 %collective-permute-start.65 = (bf16[96,768]{1,0:T(8,128)(2,1)}, bf16[96,768]{1,0:T(8,128)(2,1)}, u32[]{:S(2)}, u32[]{:S(2)}) collective-permute-start(bf16[96,768]{1,0:T(8,128)(2,1)} %fusion.82), channel_id=1, source_target_pairs={{0,2},{1,3},{2,4},{3,5},{4,6},{5,7},{6,0},{7,1},{8,10},{9,11},{10,... | collective-permute-start | bytes 442376 | tf_op jit(solution)/shard_map/ppermute | solution.py:123
  505.4 60.9 %collective-permute-start.74 = (bf16[96,768]{1,0:T(8,128)(2,1)}, bf16[96,768]{1,0:T(8,128)(2,1)}, u32[]{:S(2)}, u32[]{:S(2)}) collective-permute-start(bf16[96,768]{1,0:T(8,128)(2,1)} %fusion.79), channel_id=1, source_target_pairs={{0,2},{1,3},{2,4},{3,5},{4,6},{5,7},{6,0},{7,1},{8,10},{9,11},{10,... | collective-permute-start | bytes 442376 | tf_op jit(solution)/shard_map/ppermute | solution.py:123
  505.8 73.4 %collective-permute-start.59 = (bf16[2,96,768]{2,1,0:T(8,128)(2,1)S(1)}, bf16[2,96,768]{2,1,0:T(8,128)(2,1)}, u32[]{:S(2)}, u32[]{:S(2)}) collective-permute-start(bf16[2,96,768]{2,1,0:T(8,128)(2,1)S(1)} %fusion.70), channel_id=1, source_target_pairs={{0,16},{8,24},{16,0},{24,8},{1,17},{9,25},{17,1},{25,9},{2,18},{10... | collective-permute-start | bytes 884744 | tf_op jit(solution)/shard_map/ppermute | solution.py:129
  565.3 44.7 %collective-permute-start.40 = (bf16[1920,768]{1,0:T(8,128)(2,1)}, bf16[1920,768]{1,0:T(8,128)(2,1)S(1)}, u32[]{:S(2)}, u32[]{:S(2)}) collective-permute-start(bf16[1920,768]{1,0:T(8,128)(2,1)} %fusion.17), channel_id=1, source_target_pairs={{0,8},{8,0},{16,24},{24,16},{1,9},{9,1},{17,25},{25,17},{2,10},{10... | collective-permute-start | bytes 8847368 | tf_op jit(solution)/shard_map/ppermute | solution.py:129
  (115 other events, 1345.7 us)

commit v2 on v1

v2 whole, which is shorter than its diff:
```python
import functools
import math

import jax
import jax.numpy as jnp
from jax import lax
from jax.experimental import pallas as pl
from jax.experimental.pallas import tpu as pltpu
from jax.sharding import PartitionSpec as P

HEADS = 12


epsilon = 1e-12
scaling = 0.125


def normalize(values, gain, bias_row):
    center = values - jnp.mean(values, axis=-1, keepdims=True)
    inverse = lax.rsqrt(jnp.mean(center * center, axis=-1, keepdims=True) + epsilon)
    scaled = center * inverse
    return (scaled * gain + bias_row, scaled, inverse)


def normalize_back(upstream, scaled, inverse, gain):
    weighted = upstream * gain
    return inverse * (
        weighted
        - jnp.mean(weighted, axis=-1, keepdims=True)
        - scaled * jnp.mean(weighted * scaled, axis=-1, keepdims=True)
    )


def gelu_slope(inner):
    cumulative = 0.5 * (1.0 + lax.erf(inner * (1.0 / math.sqrt(2.0))))
    density = jnp.exp(-0.5 * inner * inner) * (1.0 / math.sqrt(2.0 * math.pi))
    return cumulative + inner * density


def matmul(left, right):
    return jnp.dot(left, right, preferred_element_type=jnp.float32)


def contract_rows(left, right):
    return jnp.einsum("ti,tj->ij", left, right, preferred_element_type=jnp.float32)


def times_transposed(left, right):
    return jnp.einsum("tj,ij->ti", left, right, preferred_element_type=jnp.float32)


def split_heads(rows):
    return rows.reshape(rows.shape[0], HEADS, rows.shape[1] // HEADS)


def masked_scores(query_heads, key_heads, visible):
    scores = (
        jnp.einsum("qhd,khd->hqk", query_heads, key_heads, preferred_element_type=jnp.float32)
        * scaling
    )
    return jnp.where(visible[None, None, :], scores, -1e30)


def attend(inputs):
    query_rows, key_rows, value_rows, visible = inputs
    query_heads = split_heads(query_rows)
    scores = masked_scores(query_heads, split_heads(key_rows), visible)
    largest = jnp.max(scores, axis=-1, keepdims=True)
    raised = jnp.exp(scores - largest)
    totals = jnp.sum(raised, axis=-1, keepdims=True)
    probs = raised / totals
    context = jnp.einsum(
        "hqk,khd->qhd",
        probs.astype(jnp.bfloat16),
        split_heads(value_rows),
        preferred_element_type=jnp.float32,
    )
    return (context.reshape(query_rows.shape).astype(jnp.bfloat16), largest + jnp.log(totals))


def attend_back(inputs):
    query_rows, key_rows, value_rows, visible, kept_lse, context_grad = inputs
    query_heads = split_heads(query_rows)
    key_heads = split_heads(key_rows)
    value_heads = split_heads(value_rows)
    grad_heads = split_heads(context_grad)
    probs = jnp.exp(masked_scores(query_heads, key_heads, visible) - kept_lse)
    prob_grad = jnp.einsum(
        "qhd,khd->hqk", grad_heads, value_heads, preferred_element_type=jnp.float32
    )
    centered = prob_grad - jnp.sum(prob_grad * probs, axis=-1, keepdims=True)
    score_grad = (probs * centered).astype(jnp.bfloat16)
    query_grad = (
        jnp.einsum("hqk,khd->qhd", score_grad, key_heads, preferred_element_type=jnp.float32)
        * scaling
    )
    key_grad = (
        jnp.einsum("hqk,qhd->khd", score_grad, query_heads, preferred_element_type=jnp.float32)
        * scaling
    )
    value_grad = jnp.einsum(
        "hqk,qhd->khd", probs.astype(jnp.bfloat16), grad_heads, preferred_element_type=jnp.float32
    )
    return (
        query_grad.reshape(query_rows.shape),
        key_grad.reshape(key_rows.shape),
        value_grad.reshape(value_rows.shape),
    )


class Links:
    def __init__(self, groups, owners):
        self.groups, self.owners = groups, owners
        self.A = 4 if owners % 4 == 0 else 1
        self.B = owners // self.A

    def place(self):
        vocab = lax.axis_index("vocab")
        return vocab // self.B, vocab % self.B

    def step_a(self, piece, far=1):
        A, B = self.A, self.B
        pairs = [(a * B + b, (a + far) % A * B + b) for a in range(A) for b in range(B)]
        return lax.ppermute(piece, "vocab", pairs)

    def step_b(self, piece):
        A, B = self.A, self.B
        pairs = [(a * B + b, a * B + (b + 1) % B) for a in range(A) for b in range(B)]
        return lax.ppermute(piece, "vocab", pairs)

    def swap(self, piece, bit):
        return lax.ppermute(piece, "dp", [(i, i ^ bit) for i in range(self.groups)])

    def row(self, piece):
        pieces = [piece]
        for _ in range(1, self.B):
            pieces.append(self.step_b(pieces[-1]))
        return pieces

    def sources(self):
        a, b = self.place()
        A, B = self.A, self.B
        return jnp.stack([(a - k + A) % A * B + (b - m + B) % B for k in range(A) for m in range(B)])

    def fold_b(self, total, axis):
        B = self.B
        here = self.place()[1]

        def block(index):
            return pick(total, index % B, axis + 1)

        held = block(here - 1 + B)
        for s in range(1, B):
            held = add(self.step_b(held), block(here - 1 - s + 2 * B))
        return held

    def fold_a(self, total, axis):
        A = self.A
        here = self.place()[0]
        terms = [pick(total, here, axis)]
        for far in range(1, A):
            terms.append(self.step_a(pick(total, (here + far) % A, axis), far))
        return add(*terms)

    def split(self, total, axis):
        return total.reshape(total.shape[:axis] + (self.A, self.B) + total.shape[axis + 1 :])

    def far(self, piece, first):
        bit = first
        while bit < self.groups:
            piece = add(piece, self.swap(piece, bit))
            bit *= 2
        return piece


def add(*terms):
    return sum(term.astype(jnp.float32) for term in terms).astype(jnp.bfloat16)


def tie(*values):
    return lax.optimization_barrier(values)


def gelu(inner):
    return inner * (0.5 * (1.0 + lax.erf(inner * (1.0 / math.sqrt(2.0)))))


def pick(stacked, index, axis=0):
    return lax.dynamic_index_in_dim(stacked, index, axis, keepdims=False)


def arrange(sources, pieces, bands, lanes):
    owners = len(pieces)

    def body(sources_ref, *refs):
        ins, outs = refs[:owners], refs[owners:]
        for i in range(owners):
            where = sources_ref[i]
            for (start, size), wide, out in zip(bands, lanes, outs):
                out[where] = ins[i][start : start + size, :wide]

    return pl.pallas_call(
        body,
        out_shape=tuple(
            jax.ShapeDtypeStruct((owners, size, wide), pieces[0].dtype)
            for (start, size), wide in zip(bands, lanes)
        ),
        in_specs=[pl.BlockSpec(memory_space=pltpu.SMEM)]
        + [pl.BlockSpec(memory_space=pltpu.VMEM)] * owners,
        out_specs=tuple(pl.BlockSpec(memory_space=pltpu.VMEM) for _ in bands),
        cost_estimate=pl.CostEstimate(
            flops=0, bytes_accessed=4 * owners * pieces[0].size, transcendentals=0
        ),
        name="arrange",
    )(sources, *pieces)


def cost(micros):
    return pl.CostEstimate(flops=0, bytes_accessed=int(micros * 3e6), transcendentals=0)


def whole(count):
    return [pl.BlockSpec(memory_space=pltpu.VMEM)] * count


SMEM = pl.BlockSpec(memory_space=pltpu.SMEM)


def dot(left, right, dims=((1,), (0,))):
    return lax.dot_general(left, right, (dims, ((), ())), preferred_element_type=jnp.float32)


def head_masks(shape):
    low = lax.broadcasted_iota(jnp.int32, shape, 1) < shape[1] // 2
    return low, jnp.logical_not(low)


def attend_kernel(length_ref, query_ref, key_ref, value_ref, context_ref):
    count, wide = query_ref.shape[0], 2 * query_ref.shape[1] // HEADS
    hidden_keys = lax.broadcasted_iota(jnp.int32, (count, count), 1) >= length_ref[0]

    @pl.loop(0, HEADS // 2)
    def _(pair):
        lanes = pl.ds(pl.multiple_of(pair * wide, wide), wide)
        query, key, value = query_ref[:, lanes], key_ref[:, lanes], value_ref[:, lanes]
        query = query * scaling
        masks = head_masks((count, wide))
        parts = []
        for mask in masks:
            scores = dot(jnp.where(mask, query, 0).astype(jnp.bfloat16), key, ((1,), (1,)))
            scores = jnp.where(hidden_keys, -1e30, scores)
            raised = jnp.exp(scores - jnp.max(scores, axis=1, keepdims=True))
            totals = jnp.sum(raised, axis=1, keepdims=True)
            parts.append(dot(raised.astype(jnp.bfloat16), value) / totals)
        context_ref[:, lanes] = jnp.where(masks[0], parts[0], parts[1]).astype(jnp.bfloat16)


def attend_call(length, query, key, value):
    return pl.pallas_call(
        attend_kernel,
        out_shape=jax.ShapeDtypeStruct(query.shape, jnp.bfloat16),
        in_specs=[SMEM] + whole(3),
        out_specs=pl.BlockSpec(memory_space=pltpu.VMEM),
        cost_estimate=cost(4),
        name="attend",
    )(length, query, key, value)


def attend_back_kernel(
    length_ref, query_ref, key_ref, value_ref, grad_ref,
    query_grad_ref, key_grad_ref, value_grad_ref, query_sum_ref, value_sum_ref,
):
    count, wide = query_ref.shape[0], 2 * query_ref.shape[1] // HEADS
    half = wide // 2
    hidden_keys = lax.broadcasted_iota(jnp.int32, (count, count), 0) >= length_ref[0]

    @pl.loop(0, HEADS // 2)
    def _(pair):
        lanes = pl.ds(pl.multiple_of(pair * wide, wide), wide)
        query, key = query_ref[:, lanes] * scaling, key_ref[:, lanes]
        query = query.astype(jnp.bfloat16)
        value, grad = value_ref[:, lanes], grad_ref[:, lanes]
        across = jnp.transpose(key.astype(jnp.float32)).astype(jnp.bfloat16)
        masks = head_masks((count, wide))
        query_parts, key_parts, value_parts = [], [], []
        for i, mask in enumerate(masks):
            scores = dot(key, jnp.where(mask, query, 0).astype(jnp.bfloat16), ((1,), (1,)))
            scores = jnp.where(hidden_keys, -1e30, scores)
            raised = jnp.exp(scores - jnp.max(scores, axis=0, keepdims=True))
            probs = raised * (1.0 / jnp.sum(raised, axis=0, keepdims=True))
            prob_grad = dot(jnp.where(mask, value, 0).astype(jnp.bfloat16), grad, ((1,), (1,)))
            centered = prob_grad - jnp.sum(prob_grad * probs, axis=0, keepdims=True)
            score_grad = (probs * centered).astype(jnp.bfloat16)
            value_parts.append(dot(probs.astype(jnp.bfloat16), grad))
            key_parts.append(dot(score_grad, query))
            query_parts.append(dot(across[i * half : (i + 1) * half], score_grad))
        value_grad = jnp.where(masks[0], value_parts[0], value_parts[1]).astype(jnp.bfloat16)
        value_grad_ref[:, lanes] = value_grad
        value_sum_ref[:, lanes] = jnp.sum(value_grad.astype(jnp.float32), axis=0, keepdims=True)
        key_grad = jnp.where(masks[0], key_parts[0], key_parts[1])
        key_grad_ref[:, lanes] = key_grad.astype(jnp.bfloat16)
        query_grad = jnp.transpose(jnp.concatenate(query_parts, axis=0) * scaling)
        query_grad = query_grad.astype(jnp.bfloat16)
        query_grad_ref[:, lanes] = query_grad
        query_sum_ref[:, lanes] = jnp.sum(query_grad.astype(jnp.float32), axis=0, keepdims=True)


def attend_back_call(length, query, key, value, grad):
    like = jax.ShapeDtypeStruct(query.shape, jnp.bfloat16)
    line = jax.ShapeDtypeStruct((1, query.shape[1]), jnp.float32)
    return pl.pallas_call(
        attend_back_kernel,
        out_shape=(like, like, like, line, line),
        in_specs=[SMEM] + whole(4),
        out_specs=tuple(whole(5)),
        cost_estimate=cost(3),
        name="attend_back",
    )(length, query, key, value, grad)


def hidden_kernel(rows_ref, shift_ref, *refs):
    inner_refs, outer_refs, active_refs, slope_refs = (refs[4 * i : 4 * i + 4] for i in range(4))
    branch_ref = refs[16]
    width = rows_ref.shape[1]
    tile = 256
    branch_ref[...] = jnp.zeros_like(branch_ref)
    for i in range(4):

        @pl.loop(0, width // tile)
        def _(part, i=i):
            lanes = pl.ds(pl.multiple_of(part * tile, tile), tile)
            inner = dot(rows_ref[...], inner_refs[i][:, lanes]) + shift_ref[i : i + 1, lanes]
            cumulative = 0.5 * (1.0 + lax.erf(inner * (1.0 / math.sqrt(2.0))))
            density = jnp.exp(-0.5 * inner * inner) * (1.0 / math.sqrt(2.0 * math.pi))
            active = (inner * cumulative).astype(jnp.bfloat16)
            active_refs[i][:, lanes] = active
            slope_refs[i][:, lanes] = (cumulative + inner * density).astype(jnp.bfloat16)
            branch_ref[...] += dot(active, outer_refs[i][lanes, :])


def hidden_call(rows, shift, inner, outer):
    like = jax.ShapeDtypeStruct(rows.shape, jnp.bfloat16)
    out = pl.pallas_call(
        hidden_kernel,
        out_shape=(like,) * 8 + (jax.ShapeDtypeStruct(rows.shape, jnp.float32),),
        in_specs=whole(10),
        out_specs=tuple(whole(9)),
        cost_estimate=cost(8),
        name="hidden",
    )(rows, shift, *inner, *outer)
    return out[:4], out[4:8], out[8]


def widen_kernel(core_ref, here_ref, there_ref, out_ref):
    wide = here_ref.shape[1]

    @pl.when(core_ref[0] == 0)
    def _():
        out_ref[:, :wide] = here_ref[...].astype(jnp.float32)
        out_ref[:, wide:] = there_ref[...].astype(jnp.float32)

    @pl.when(core_ref[0] != 0)
    def _():
        out_ref[:, :wide] = there_ref[...].astype(jnp.float32)
        out_ref[:, wide:] = here_ref[...].astype(jnp.float32)


def widen_call(core, here, there):
    count, wide = here.shape
    tile = count // 8
    return pl.pallas_call(
        widen_kernel,
        grid=(8,),
        out_shape=jax.ShapeDtypeStruct((count, 2 * wide), jnp.float32),
        in_specs=[SMEM] + [pl.BlockSpec((tile, wide), lambda i: (i, 0))] * 2,
        out_specs=pl.BlockSpec((tile, 2 * wide), lambda i: (i, 0)),
        cost_estimate=cost(5),
        name="widen",
    )(core.reshape(1), here, there)


def on_device(
    groups,
    owners,
    token_ids,
    lengths,
    word_table,
    position_table,
    embed_gain,
    embed_bias,
    query_weight,
    query_bias,
    key_weight,
    value_weight,
    value_bias,
    output_weight,
    output_bias,
    middle_gain,
    middle_bias,
    inner_weight,
    inner_bias,
    outer_weight,
    outer_bias,
    final_gain,
    final_bias,
    cotangent,
):
    links = Links(groups, owners)
    table_rows, width = word_table.shape
    full_len = token_ids.shape[1]
    rows = query_weight.shape[0]
    hidden = inner_weight.shape[1]
    cap = 2 * full_len // owners
    place_part = position_table.shape[0] // 2
    dp = lax.axis_index("dp")
    core, quarter = dp % 2, dp % 4
    blocks = [quarter, quarter ^ 1, quarter ^ 2, quarter ^ 3]
    ids = token_ids.reshape(full_len)

    inner_quarter = pick(inner_weight.reshape(rows, owners, 4, rows), quarter, 2)
    hidden_piece = jnp.concatenate(
        [
            inner_quarter.reshape(rows, width),
            lax.dynamic_slice_in_dim(outer_weight, quarter * rows, rows, 0),
        ]
    )
    vectors = [
        embed_gain, embed_bias, query_bias, value_bias, output_bias, middle_gain, middle_bias,
        outer_bias, final_gain, final_bias,
    ]
    vectors += [inner_bias[i * rows : (i + 1) * rows] for i in range(4)]
    vector_piece = sum(
        lax.pad(
            item.reshape(1, rows),
            jnp.zeros((), jnp.bfloat16),
            ((i, 15 - i, 0), (0, width - rows, 0)),
        )
        for i, item in enumerate(vectors)
    )
    square_piece = jnp.concatenate(
        [
            jnp.where(core == 0, query_weight, value_weight),
            jnp.where(core == 0, key_weight, output_weight),
            lax.dynamic_slice_in_dim(position_table, core * place_part, place_part, 0),
            vector_piece,
        ]
    )

    owner = ids // table_rows
    local = ids - owner * table_rows
    onehot = owner[:, None] == lax.iota(jnp.int32, owners)[None, :]
    before = lax.iota(jnp.int32, full_len)
    lower = (before[:, None] > before[None, :]).astype(jnp.bfloat16)
    ranks = matmul(lower, onehot.astype(jnp.bfloat16))
    rank = jnp.sum(jnp.where(onehot, ranks, 0.0), axis=1).astype(jnp.int32)
    slot = owner * cap + rank
    slots = lax.iota(jnp.int32, owners * cap)
    sent_ids = jnp.sum(
        jnp.where(slots[:, None] == slot[None, :], local[None, :] + 1, 0), axis=1
    ) - 1
    held_ids = lax.all_to_all(sent_ids.reshape(owners, cap), "vocab", 0, 0, tiled=True).reshape(-1)

    picked = jnp.take(word_table, jnp.maximum(held_ids, 0), axis=0)
    hidden_pieces, square_pieces, beyond_pieces = [], [], []
    hidden_held, square_held = hidden_piece, square_piece
    A = links.A
    plan = [(0, 0, None), (1, None, 0), (2, 1, None), (3, 2, 1)]
    if A == 1:
        plan = [(0, None, None)]
    arrived = None
    for square_step, hidden_step, cross in plan:
        square_row = links.row(square_held)
        square_next = links.step_a(square_held) if square_step < A - 1 else ()
        hidden_row, hidden_next, crossing = (), (), ()
        if hidden_step is not None:
            hidden_row, hidden_next = links.row(hidden_held), links.step_a(hidden_held)
        if cross is not None:
            here = slice(cross * links.B, (cross + 1) * links.B)
            crossing = [links.swap(piece, 2) for piece in hidden_pieces[here]]
        tied = tie(square_row, square_next, hidden_row, hidden_next, crossing, picked)
        square_row, square_next, hidden_row, hidden_next, crossing, picked = tied
        square_pieces += square_row
        hidden_pieces += hidden_row
        beyond_pieces += crossing
        square_held = square_next
        if hidden_step is not None:
            hidden_held = hidden_next
        if arrived is None:
            arrived = lax.all_to_all(
                picked.reshape(owners, cap, width), "vocab", 0, 0, tiled=True
            )
    sources = links.sources()
    first_here, second_here, place_here, small = arrange(
        sources,
        square_pieces,
        [(0, rows), (rows, rows), (2 * rows, place_part), (2 * rows + place_part, 16)],
        [width, width, width, 128 * -(-rows // 128)],
    )
    first_there, second_there, place_there = (
        links.swap(item, 1) for item in (first_here, second_here, place_here)
    )
    hidden_row = links.row(hidden_held)
    first_cross = [links.swap(p, 2) for p in hidden_pieces[len(beyond_pieces) :]]

    small = jnp.transpose(small[:, :, :rows], (1, 0, 2)).reshape(16, width).astype(jnp.float32)
    (
        embed_scale, embed_shift, query_shift, value_shift, output_shift, middle_scale,
        middle_shift, outer_shift, final_scale, final_shift,
    ) = (small[i] for i in range(10))
    inner_shift = jnp.stack([pick(small, 10 + i) for i in blocks])

    def ordered(here, there):
        return jnp.where(core == 0, here, there), jnp.where(core == 0, there, here)

    query_matrix, value_matrix = ordered(
        first_here.reshape(width, width), first_there.reshape(width, width)
    )
    key_matrix, output_matrix = ordered(
        second_here.reshape(width, width), second_there.reshape(width, width)
    )
    place_rows = jnp.stack(ordered(place_here, place_there), axis=1).reshape(full_len, width)

    route = (slot[:, None] == slots[None, :]).astype(jnp.bfloat16)
    embedded = matmul(route, arrived.reshape(owners * cap, width))
    summed = embedded + place_rows.astype(jnp.float32)
    normed, hat_embed, inv_embed = normalize(summed, embed_scale, embed_shift)
    normed_low = normed.astype(jnp.bfloat16)
    query_low = (matmul(normed_low, query_matrix) + query_shift).astype(jnp.bfloat16)
    key_low = matmul(normed_low, key_matrix).astype(jnp.bfloat16)
    value_low = (matmul(normed_low, value_matrix) + value_shift).astype(jnp.bfloat16)
    query_low, hidden_row, first_cross = tie(query_low, hidden_row, first_cross)
    hidden_pieces += hidden_row
    beyond_pieces += first_cross
    last_cross = [links.swap(p, 2) for p in hidden_pieces[len(beyond_pieces) :]]
    inner_here, outer_here = arrange(
        sources, hidden_pieces, [(0, rows), (rows, rows)], [width, width]
    )
    inner_beside, outer_beside = links.swap(inner_here, 1), links.swap(outer_here, 1)
    context = attend_call(lengths, query_low, key_low, value_low)
    context, last_cross = tie(context, last_cross)
    beyond_pieces += last_cross
    inner_beyond, outer_beyond = arrange(
        sources, beyond_pieces, [(0, rows), (rows, rows)], [width, width]
    )
    inner_matrix = [inner_here, inner_beside, inner_beyond, links.swap(inner_beyond, 1)]
    outer_matrix = [outer_here, outer_beside, outer_beyond, links.swap(outer_beyond, 1)]
    inner_matrix = [item.reshape(width, width) for item in inner_matrix]
    outer_matrix = [item.reshape(width, width) for item in outer_matrix]
    attended = matmul(context, output_matrix) + output_shift
    middle, hat_middle, inv_middle = normalize(normed + attended, middle_scale, middle_shift)
    middle_low = middle.astype(jnp.bfloat16)
    activated, slopes, branch = hidden_call(middle_low, inner_shift, inner_matrix, outer_matrix)
    result, hat_final, inv_final = normalize(
        middle + branch + outer_shift, final_scale, final_shift
    )
    output = result.astype(jnp.bfloat16).reshape(1, full_len, width)

    upstream = cotangent.reshape(full_len, width).astype(jnp.float32)
    final_gain_gradient = jnp.sum(upstream * hat_final, axis=0)
    final_bias_gradient = jnp.sum(upstream, axis=0)
    second = normalize_back(upstream, hat_final, inv_final, final_scale)
    branch_grad = second.astype(jnp.bfloat16)
    outer_bias_gradient = jnp.sum(branch_grad.astype(jnp.float32), axis=0)

    def local_terms(left, right):
        return contract_rows(left, right).astype(jnp.bfloat16).reshape(owners, rows, width)

    outer_terms = [None] * 4
    for i in (3, 1, 2, 0):
        outer_terms[i] = local_terms(activated[i], branch_grad)
    outer_cross = [links.swap(outer_terms[i], 1) for i in (3, 1)]
    inner_grad = [
        (times_transposed(branch_grad, outer_matrix[i]) * slopes[i].astype(jnp.float32)).astype(jnp.bfloat16)
        for i in range(4)
    ]
    inner_grad, outer_cross = tie(inner_grad, outer_cross)
    outer_sent, inner_grad = tie(add(outer_terms[2], outer_cross[0]), inner_grad)
    outer_across = links.swap(outer_sent, 2)
    outer_near = add(outer_terms[0], outer_cross[1])
    inner_bias_gradient = [jnp.sum(item.astype(jnp.float32), axis=0) for item in inner_grad]
    inner_terms = [None] * 4
    for i in (3, 1, 2, 0):
        inner_terms[i] = contract_rows(middle_low, inner_grad[i]).astype(jnp.bfloat16)
        inner_terms[i] = inner_terms[i].reshape(owners, rows, width)
    inner_cross = [links.swap(inner_terms[i], 1) for i in (3, 1)]
    middle_grad = second + sum(times_transposed(inner_grad[i], inner_matrix[i]) for i in range(4))
    middle_grad, inner_cross, outer_across = tie(middle_grad, inner_cross, outer_across)
    inner_across_sent, outer_whole, middle_grad = tie(
        add(inner_terms[2], inner_cross[0]),
        links.split(add(outer_near, outer_across), 0),
        middle_grad,
    )
    inner_across = links.swap(inner_across_sent, 2)
    outer_half = links.fold_b(outer_whole, 0)
    inner_near = add(inner_terms[0], inner_cross[1])
    middle_gain_gradient = jnp.sum(middle_grad * hat_middle, axis=0)
    middle_bias_gradient = jnp.sum(middle_grad, axis=0)
    first = normalize_back(middle_grad, hat_middle, inv_middle, middle_scale)
    attended_grad = first.astype(jnp.bfloat16)
    output_bias_gradient = jnp.sum(attended_grad.astype(jnp.float32), axis=0)
    context_grad = times_transposed(attended_grad, output_matrix).astype(jnp.bfloat16)
    query_low_grad, key_low_grad, value_low_grad, query_bias_gradient, value_bias_gradient = (
        attend_back_call(lengths, query_low, key_low, value_low, context_grad)
    )
    query_low_grad, key_low_grad, value_low_grad, inner_across, outer_half = tie(
        query_low_grad, key_low_grad, value_low_grad, inner_across, outer_half
    )
    outer_share = links.fold_a(outer_half, 0)
    inner_half = links.fold_b(links.split(add(inner_near, inner_across), 0), 0)
    own_left = jnp.where(core == 0, normed_low, context)
    sent_left = jnp.where(core == 0, context, normed_low)
    square_sent = [
        local_terms(normed_low, jnp.where(core == 0, value_low_grad, query_low_grad)),
        local_terms(sent_left, jnp.where(core == 0, attended_grad, key_low_grad)),
    ]
    square_cross = [links.swap(item, 1) for item in square_sent]
    square_own = [
        local_terms(normed_low, jnp.where(core == 0, query_low_grad, value_low_grad)),
        local_terms(own_left, jnp.where(core == 0, key_low_grad, attended_grad)),
    ]
    normed_grad = (
        first
        + times_transposed(query_low_grad, query_matrix)
        + times_transposed(key_low_grad, key_matrix)
        + times_transposed(value_low_grad, value_matrix)
    )
    embed_gain_gradient = jnp.sum(normed_grad * hat_embed, axis=0)
    embed_bias_gradient = jnp.sum(normed_grad, axis=0)
    summed_grad = normalize_back(normed_grad, hat_embed, inv_embed, embed_scale)
    embedded_grad = summed_grad.astype(jnp.bfloat16)
    embedded_grad, outer_share, inner_half, square_cross = tie(
        embedded_grad, outer_share, inner_half, square_cross
    )

    wide = width // 2
    features = [embedded_grad[:, :wide], embedded_grad[:, wide:]]

    def rows_of(features):
        return jnp.einsum(
            "ts,td->sd", route, features, preferred_element_type=jnp.float32
        ).astype(jnp.bfloat16)

    kept = rows_of(jnp.where(core == 0, features[0], features[1]))
    given = links.swap(rows_of(jnp.where(core == 0, features[1], features[0])), 1)
    leaving = jnp.stack(
        [item.reshape(owners, cap, wide) for item in ordered(kept, given)], axis=1
    )
    known = jnp.stack(
        [item.reshape(owners, cap) for item in ordered(held_ids, links.swap(held_ids, 1))], axis=1
    )
    parts = 2
    cut = cap // parts
    known = known.reshape(owners, 2, parts, cut).transpose(2, 0, 1, 3).reshape(-1)
    known_sets = [known]
    bit = 2
    while bit < groups:
        known_sets += [links.swap(item, bit) for item in known_sets]
        bit *= 2
    sums = [
        embed_gain_gradient, embed_bias_gradient, query_bias_gradient, value_bias_gradient,
        output_bias_gradient, middle_gain_gradient, middle_bias_gradient, outer_bias_gradient,
        final_gain_gradient, final_bias_gradient,
    ]
    inner_bias_gradient = jnp.stack(inner_bias_gradient)[jnp.stack(blocks)]
    vector_terms = jnp.concatenate(
        [item.reshape(1, width) for item in sums] + [inner_bias_gradient]
    )
    vector_terms = vector_terms.reshape(14, owners, rows).transpose(1, 0, 2)
    vector_terms = jnp.pad(vector_terms, ((0, 0), (0, 2), (0, width - rows)))
    vector_terms = vector_terms.reshape(owners, 2, 8, width).astype(jnp.bfloat16)
    place_terms = embedded_grad.reshape(owners, 2, place_part, width)
    late_terms = jnp.concatenate([place_terms, vector_terms], axis=2)
    late_cross = links.swap(pick(late_terms, 1 - core, 1), 1)
    bits = []
    bit = 2
    while bit < groups:
        bits.append(bit)
        bit *= 2

    def exchange(part):
        piece = leaving[:, :, part * cut : (part + 1) * cut]
        return lax.all_to_all(piece, "vocab", 0, 0, tiled=True)

    def beyond(piece):
        items = [piece]
        for bit in bits:
            items = items + [links.swap(item, bit) for item in items]
        return items

    def table_term(pieces, known):
        return matmul((table_ids[:, None] == known[None, :]).astype(jnp.bfloat16), pieces)

    table_ids = lax.iota(jnp.int32, table_rows)
    landed, late_cross, leaving = tie(exchange(0).reshape(-1, wide), late_cross, leaving)
    late_whole = jnp.concatenate(
        [
            add(square_own[0], square_cross[0]),
            add(square_own[1], square_cross[1]),
            add(pick(late_terms, core, 1), late_cross),
        ],
        axis=1,
    )
    late_half = links.fold_b(links.split(late_whole, 0), 0)
    first_sets = beyond(landed)
    landed, late_half, first_sets = tie(exchange(1).reshape(-1, wide), late_half, first_sets)
    share = links.fold_a(jnp.concatenate([inner_half, late_half], axis=1), 0)
    second_sets = beyond(landed)
    table_sum = [table_term(jnp.concatenate([first_sets[0], second_sets[0]]), known_sets[0])]
    share, second_sets, table_sum = tie(share, second_sets, table_sum)
    share = links.far(jnp.concatenate([outer_share, share]), 4)
    share_beyond = links.swap(share, 2)
    for i in range(1, len(known_sets)):
        pieces = jnp.concatenate([first_sets[i], second_sets[i]])
        table_sum.append(table_term(pieces, known_sets[i]))
    while len(table_sum) > 1:
        table_sum = [a + b for a, b in zip(table_sum[::2], table_sum[1::2])]
    table_half, share_beyond = tie(table_sum[0].astype(jnp.bfloat16), share_beyond)
    late_share = add(share[2 * rows :], share_beyond[2 * rows :])
    share_core = jnp.concatenate([share[: 2 * rows], share_beyond[: 2 * rows], late_share])
    table_other, share_other = links.swap(table_half, 1), links.swap(share_core, 1)
    table_other, share_other = tie(table_other, share_other)
    table_gradient = widen_call(core, table_half, table_other)
    low_share, high_share = ordered(share_core[4 * rows :], share_other[4 * rows :])
    first_share, second_share = low_share[:rows], low_share[rows : 2 * rows]
    third_share, fourth_share = high_share[:rows], high_share[rows : 2 * rows]
    place_end = 2 * rows + place_part
    position_gradient = jnp.concatenate(
        [low_share[2 * rows : place_end], high_share[2 * rows : place_end]]
    )
    vector_share = jnp.concatenate([low_share[place_end:, :rows], high_share[place_end:, :rows]])
    vector_share = vector_share.astype(jnp.float32)
    (
        embed_gain_gradient, embed_bias_gradient, query_bias_gradient, value_bias_gradient,
        output_bias_gradient, middle_gain_gradient, middle_bias_gradient, outer_bias_gradient,
        final_gain_gradient, final_bias_gradient,
    ) = (vector_share[i] for i in range(10))
    inner_bias_gradient = vector_share[10:14].reshape(4 * rows)

    def quad(start):
        own, beside = share_core[start : start + 3 * rows], share_other[start : start + 3 * rows]
        items = [own[:rows], beside[:rows], own[2 * rows :], beside[2 * rows :]]
        return jnp.stack(items)[jnp.stack(blocks)]

    outer_weight_gradient = quad(0).reshape(4 * rows, width)
    inner_weight_gradient = quad(rows).reshape(4, rows, owners, rows)
    inner_weight_gradient = inner_weight_gradient.transpose(1, 2, 0, 3).reshape(rows, hidden)

    def wider(share):
        return share.astype(jnp.float32)

    return (
        output,
        table_gradient,
        wider(position_gradient),
        embed_gain_gradient,
        embed_bias_gradient,
        wider(first_share),
        query_bias_gradient,
        wider(second_share),
        wider(third_share),
        value_bias_gradient,
        wider(fourth_share),
        output_bias_gradient,
        middle_gain_gradient,
        middle_bias_gradient,
        wider(inner_weight_gradient),
        inner_bias_gradient,
        wider(outer_weight_gradient),
        outer_bias_gradient,
        final_gain_gradient,
        final_bias_gradient,
    )


def solution(mesh):
    return jax.shard_map(
        functools.partial(on_device, mesh.shape["dp"], mesh.shape["vocab"]),
        mesh=mesh,
        in_specs=(
            P(("dp", "vocab"), None),
            P(("dp", "vocab")),
            P("vocab", None),
            P("vocab", None),
            P("vocab"),
            P("vocab"),
            P("vocab", None),
            P("vocab"),
            P("vocab", None),
            P("vocab", None),
            P("vocab"),
            P("vocab", None),
            P("vocab"),
            P("vocab"),
            P("vocab"),
            P("vocab", None),
            P("vocab"),
            P("vocab", None),
            P("vocab"),
            P("vocab"),
            P("vocab"),
            P(("dp", "vocab"), None, None),
        ),
        out_specs=(
            P(("dp", "vocab"), None, None),
            P("vocab", None),
            P("vocab", None),
            P("vocab"),
            P("vocab"),
            P("vocab", None),
            P("vocab"),
            P("vocab", None),
            P("vocab", None),
            P("vocab"),
            P("vocab", None),
            P("vocab"),
            P("vocab"),
            P("vocab"),
            P("vocab", None),
            P("vocab"),
            P("vocab", None),
            P("vocab"),
            P("vocab"),
            P("vocab"),
        ),
        check_vma=False,
    )
```

time: 627 us -> 472 us (0.75)
  waiting for transfers between devices: 225 us -> 151 us
  local copies, waits for them, and re-layouts: 119 us -> 49.6 us
  Pallas kernels: 0 us -> 63.6 us
  matrix products: 124 us -> 70.8 us
  starting transfers between devices: 89 us -> 78.3 us
  other arithmetic: 57.6 us -> 48.1 us
    pallas_call x0 -> x7, Pallas kernels: none -> 63.6 us  [the longest x1 19.3 us: hidden_call(): pl.pallas_call(hidden_kernel, out_shape=(like,) * 8 + (jax.ShapeDtypeStru...]
    dynamic_update_slice x51 -> x0, local copies, waits for them, and re-layouts: 58.1 us -> none  [the longest x21 41.2 us: put(): out = lax.dynamic_update_index_in_dim(out, block, index, axis)]
    ppermute x31 -> x32, waiting for transfers between devices: 87.5 us -> 37.7 us  [swap(): return lax.ppermute(piece, 'dp', [(i, i ^ bit) for i in range(self.groups)])]
    ppermute x48 -> x23, waiting for transfers between devices: 138 us -> 104 us  [the longest x12 74.4 us: step_a(): return lax.ppermute(piece, 'vocab', pairs)]
    dot_general x7 -> x2, matrix products: 29.2 us -> 1.68 us  [rows_of(): jnp.einsum('ts,td->sd', route, features, preferred_element_type=jnp.float32)]
    ppermute x48 -> x23, starting transfers between devices: 60.6 us -> 40.7 us  [the longest x12 28.8 us: step_a(): return lax.ppermute(piece, 'vocab', pairs)]
    dot_general x9 -> x12, matrix products: 32.7 us -> 20.8 us  [times_transposed(): jnp.einsum('tj,ij->ti', left, right, preferred_element_type=jnp.float32)]
    broadcast_in_dim x12 -> x0, local copies, waits for them, and re-layouts: 11.9 us -> none  [the longest x8 9.73 us: put(): out = jnp.zeros(shape, blocks[0].dtype)]
  transfers between devices with their start and end apart: 82 -> 59, of which waited for: 27 -> 18; matrix products, arithmetic and copies ran while one was open for 24% -> 23% of each run, Pallas kernels for 0% -> 8%
where the time goes in v2:
time: 472 us; the launch traced here: 465 us
  waiting for transfers between devices  151 us (32%)
  starting transfers between devices  78.3 us (17%)
  matrix products  70.8 us (15%)
  Pallas kernels  63.6 us (13%)
  local copies, waits for them, and re-layouts  49.6 us (11%)
  other arithmetic  48.1 us (10%)
    ppermute x12, waiting for transfers between devices, step_a(): return lax.ppermute(piece, 'vocab', pairs)  74.4 us
    ppermute x32, waiting for transfers between devices, swap(): return lax.ppermute(piece, 'dp', [(i, i ^ bit) for i in range(self.groups)])  37.7 us
    dot_general x8, matrix products, matmul(): return jnp.dot(left, right, preferred_element_type=jnp.float32)  32.2 us
    ppermute x11, waiting for transfers between devices, step_b(): return lax.ppermute(piece, 'vocab', pairs)  29.8 us
    ppermute x12, starting transfers between devices, step_a(): return lax.ppermute(piece, 'vocab', pairs)  28.8 us
    dot_general x12, matrix products, times_transposed(): jnp.einsum('tj,ij->ti', left, right, preferred_element_type=jnp.float32)  20.8 us
    ppermute x32, starting transfers between devices, swap(): return lax.ppermute(piece, 'dp', [(i, i ^ bit) for i in range(self.groups)])  20.1 us
    pallas_call x1, Pallas kernels, hidden_call(): pl.pallas_call(hidden_kernel, out_shape=(like,) * 8 + (jax.ShapeDtypeStru...  19.3 us
  transfers between devices with their start and end apart: 59, of which 18 were waited for; matrix products, arithmetic and copies ran while one was open for 23% of the time, Pallas kernels for 8%

profile of v2, /device:TPU:0, one launch (start us, length us, event | category | flops | bytes accessed | tf_op | source)
XLA Modules:
  0.0 464.6 jit_solution(12554707891646063439)
XLA Ops:
  10.2 3.9 all-to-all-start
  20.5 7.9 %gather_fusion = bf16[1024,768]{1,0:T(8,128)(2,1)S(1)} fusion(bf16[3840,768]{1,0:T(8,128)(2,1)} %param.24, s32[1024]{0:T(1024)S(1)} %broadcast_clamp_fusion), kind=kCustom, calls=%fused_computation | custom fusion | bytes 3149824 | tf_op jit(solution)/shard_map/jit(_take)/gather | solution.py:463
  33.4 5.2 %all-to-all-start.1 = ((bf16[8,128,768]{2,1,0:T(8,128)(2,1)}), bf16[8,128,768]{2,1,0:T(8,128)(2,1)S(1)}, u32[]{:S(2)}, u32[]{:S(2)}) async-start(bf16[8,128,768]{2,1,0:T(8,128)(2,1)} %bitcast.21), calls=%async_computation.1 | async-start | bytes 3145728 | tf_op jit(solution)/shard_map/all_to_all | solution.py:489
  48.2 31.9 %collective-permute-done.11.refs_4_ = bf16[192,768]{1,0:T(8,128)(2,1)} collective-permute-done((bf16[192,768]{1,0:T(8,128)(2,1)}, bf16[192,768]{1,0:T(8,128)(2,1)}, u32[]{:S(2)}, u32[]{:S(2)}) %collective-permute-start.11) | collective-permute-done | bytes 294944 | tf_op jit(solution)/shard_map/ppermute | solution.py:124
  83.9 6.5 %collective-permute-start.14 = (bf16[192,768]{1,0:T(8,128)(2,1)}, bf16[192,768]{1,0:T(8,128)(2,1)}, u32[]{:S(2)}, u32[]{:S(2)}) collective-permute-start(bf16[192,768]{1,0:T(8,128)(2,1)} %collective-permute-done.11.refs_4_), channel_id=1, source_target_pairs={{0,2},{1,3},{2,4},{3,5},{4,6},{5,7},{6,0},{7,1},{8,10},{9,11},{10,... | collective-permute-start | bytes 884744 | tf_op jit(solution)/shard_map/ppermute | solution.py:124
  134.7 9.2 %attend.1 = bf16[512,768]{1,0:T(8,128)(2,1)} custom-call(s32[1]{0:T(128)S(6)} %copy.122.length_ref, bf16[512,768]{1,0:T(8,128)(2,1)} %add_convert_fusion.5.query_ref, bf16[512,768]{1,0:T(8,128)(2,1)} %convolution_convert_fusion.13.key_ref, bf16[512,768]{1,0:T(8,128)(2,1)} %add_convert_fusion.4.value_ref), custom_call_target="tpu_custom_call" | custom-call | bytes 12000000 | tf_op jit(solution)/shard_map/attend/pallas_call | solution.py:259
  152.6 19.3 %hidden.1 = (bf16[512,768]{1,0:T(8,128)(2,1)}, bf16[512,768]{1,0:T(8,128)(2,1)}, bf16[512,768]{1,0:T(8,128)(2,1)}, bf16[512,768]{1,0:T(8,128)(2,1)}, bf16[512,76...) custom-call(bf16[512,768]{1,0:T(8,128)(2,1)} %fusion.30.rows_ref, ...), custom_call_target="tpu_custom_call" | custom-call | bytes 24000000 | tf_op jit(solution)/shard_map/hidden/pallas_call | solution.py:343
  210.9 19.6 %collective-permute-done.33 = bf16[8,96,768]{2,1,0:T(8,128)(2,1)S(1)} collective-permute-done((bf16[8,96,768]{2,1,0:T(8,128)(2,1)S(1)}, bf16[8,96,768]{2,1,0:T(8,128)(2,1)S(1)}, u32[]{:S(2)}, u32[]{:S(2)}) %collective-permute-start.33) | collective-permute-done | bytes 1179680 | tf_op jit(solution)/shard_map/ppermute | solution.py:132
  240.4 16.9 %attend_back.1 = (bf16[512,768]{1,0:T(8,128)(2,1)}, bf16[512,768]{1,0:T(8,128)(2,1)}, bf16[512,768]{1,0:T(8,128)(2,1)}, f32[1,768]{1,0:T(1,128)}, f32[1,768]{1,0:T(1,128)}) custom-call(s32[1]{0:T(128)S(6)} %copy.122.length_ref, bf16[512,768]{1,0:T(8,128)(2,1)} %add_convert_fusion.5.query_ref, bf16[512,768]{1,0:T(8,128)(2,1)} %convolution_convert_fusion.13.key_ref, ...), custom_call_target="tpu_custom_call" | custom-call | bytes 9000000 | tf_op jit(solution)/shard_map/attend_back/pallas_call | solution.py:311
  265.3 6.4 %collective-permute-start.36 = (bf16[96,768]{1,0:T(8,128)(2,1)S(1)}, bf16[96,768]{1,0:T(8,128)(2,1)S(1)}, u32[]{:S(2)}, u32[]{:S(2)}) collective-permute-start(bf16[96,768]{1,0:T(8,128)(2,1)S(1)} %get-tuple-element.265), channel_id=1, source_target_pairs={{0,2},{1,3},{2,4},{3,5},{4,6},{5,7},{6,0},{7,1},{8,10},{9,11},{10,... | collective-permute-start | bytes 442376 | tf_op jit(solution)/shard_map/ppermute | solution.py:124
  277.3 3.7 collective-permute-start.37
  283.6 7.5 %collective-permute-done.37 = bf16[96,768]{1,0:T(8,128)(2,1)S(1)} collective-permute-done((bf16[96,768]{1,0:T(8,128)(2,1)S(1)}, bf16[96,768]{1,0:T(8,128)(2,1)S(1)}, u32[]{:S(2)}, u32[]{:S(2)}) %collective-permute-start.37) | collective-permute-done | bytes 147488 | tf_op jit(solution)/shard_map/ppermute | solution.py:124
  298.8 4.2 all-to-all-start.2
  314.7 8.5 %all-to-all-done.2 = bf16[8,2,64,384]{3,2,1,0:T(8,128)(2,1)} async-done(((bf16[8,2,64,384]{3,2,1,0:T(8,128)(2,1)}), bf16[8,2,64,384]{3,2,1,0:T(8,128)(2,1)}, u32[]{:S(2)}, u32[]{:S(2)}) %all-to-all-start.2) | async-done | bytes 786464 | tf_op jit(solution)/shard_map/all_to_all | solution.py:682
  329.7 4.2 all-to-all-start.3
  339.3 27.6 %collective-permute-done.44 = bf16[4,232,768]{2,1,0:T(8,128)(2,1)} collective-permute-done((bf16[4,232,768]{2,1,0:T(8,128)(2,1)}, bf16[4,232,768]{2,1,0:T(8,128)(2,1)}, u32[]{:S(2)}, u32[]{:S(2)}) %collective-permute-start.44) | collective-permute-done | bytes 1425440 | tf_op jit(solution)/shard_map/ppermute | solution.py:129
  375.2 4.0 collective-permute-start.48
  379.3 9.9 %fusion = f32[3840,384]{1,0:T(8,128)S(1)} fusion(s32[2048]{0:T(1024)S(1)} %eq.140, bf16[1024,384]{1,0:T(8,128)(2,1)} %bitcast.85, bf16[1024,384]{1,0:T(8,128)(2,1)} %bitcast.74), kind=kOutput, calls=%fused_computation.6 | convolution fusion | flops 6050807808 | bytes 7479296 | tf_op jit(solution)/shard_map/dot_general | solution.py:41
  391.4 6.6 %collective-permute-done.48 = bf16[328,768]{1,0:T(8,128)(2,1)S(1)} collective-permute-done((bf16[328,768]{1,0:T(8,128)(2,1)S(1)}, bf16[328,768]{1,0:T(8,128)(2,1)S(1)}, u32[]{:S(2)}, u32[]{:S(2)}) %collective-permute-start.48) | collective-permute-done | bytes 503840 | tf_op jit(solution)/shard_map/ppermute | solution.py:124
  398.0 21.4 %collective-permute-done.47 = bf16[328,768]{1,0:T(8,128)(2,1)S(1)} collective-permute-done((bf16[328,768]{1,0:T(8,128)(2,1)S(1)}, bf16[328,768]{1,0:T(8,128)(2,1)S(1)}, u32[]{:S(2)}, u32[]{:S(2)}) %collective-permute-start.47) | collective-permute-done | bytes 503840 | tf_op jit(solution)/shard_map/ppermute | solution.py:124
  421.4 10.0 %fusion.1 = f32[3840,384]{1,0:T(8,128)S(1)} fusion(s32[2048]{0:T(1024)S(1)} %collective-permute-done.51, bf16[1024,384]{1,0:T(8,128)(2,1)S(1)} %collective-permute-done.49, bf16[1024,384]{1,0:T(8,128)(2,1)} %collective-permute-done.45), kind=kOutput, calls=%fused_computation.7 | convolution fusion | flops 6050807808 | bytes 7479296 | tf_op jit(solution)/shard_map/dot_general | solution.py:41
  432.2 5.2 %collective-permute-done.52 = bf16[424,768]{1,0:T(8,128)(2,1)S(1)} collective-permute-done((bf16[424,768]{1,0:T(8,128)(2,1)S(1)}, bf16[424,768]{1,0:T(8,128)(2,1)S(1)}, u32[]{:S(2)}, u32[]{:S(2)}) %collective-permute-start.52) | collective-permute-done | bytes 651296 | tf_op jit(solution)/shard_map/ppermute | solution.py:132
  439.6 4.6 collective-permute-done.54
  455.7 8.5 %widen.1 = f32[3840,768]{1,0:T(8,128)} custom-call(s32[1]{0:T(128)} %bitcast.48.core_ref, bf16[3840,384]{1,0:T(8,128)(2,1)} %copy-done.7, bf16[3840,384]{1,0:T(8,128)(2,1)} %copy-done.16), custom_call_target="tpu_custom_call" | custom-call | bytes 15000000 | tf_op jit(solution)/shard_map/widen/pallas_call | solution.py:371
  (448 shorter events, 208.9 us)
Async XLA Ops:
  4.3 25.5 %collective-permute-start.1 = (bf16[240,768]{1,0:T(8,128)(2,1)S(1)}, bf16[240,768]{1,0:T(8,128)(2,1)}, u32[]{:S(2)}, u32[]{:S(2)}) collective-permute-start(bf16[240,768]{1,0:T(8,128)(2,1)S(1)} %pad_maximum_fusion.5.refs_0_), channel_id=1, source_target_pairs={{0,2},{1,3},{2,4},{3,5},{4,6},{5,7},{6,0},{7,1},{8,10},{9,11},{10,... | collective-permute-start | bytes 1105928 | tf_op jit(solution)/shard_map/ppermute | solution.py:124
  7.4 22.4 %collective-permute-start = (bf16[240,768]{1,0:T(8,128)(2,1)S(1)}, bf16[240,768]{1,0:T(8,128)(2,1)S(1)}, u32[]{:S(2)}, u32[]{:S(2)}) collective-permute-start(bf16[240,768]{1,0:T(8,128)(2,1)S(1)} %pad_maximum_fusion.5.refs_0_), channel_id=1, source_target_pairs={{0,1},{1,0},{2,3},{3,2},{4,5},{5,4},{6,7},{7,6},{8,9},{9,8},{10,11... | collective-permute-start | bytes 1105928 | tf_op jit(solution)/shard_map/ppermute | solution.py:129
  33.4 82.5 %all-to-all-start.1 = ((bf16[8,128,768]{2,1,0:T(8,128)(2,1)}), bf16[8,128,768]{2,1,0:T(8,128)(2,1)S(1)}, u32[]{:S(2)}, u32[]{:S(2)}) async-start(bf16[8,128,768]{2,1,0:T(8,128)(2,1)} %bitcast.21), calls=%async_computation.1 | async-start | bytes 3145728 | tf_op jit(solution)/shard_map/all_to_all | solution.py:489
  44.3 35.8 %collective-permute-start.9 = (bf16[240,768]{1,0:T(8,128)(2,1)S(1)}, bf16[240,768]{1,0:T(8,128)(2,1)S(1)}, u32[]{:S(2)}, u32[]{:S(2)}) collective-permute-start(bf16[240,768]{1,0:T(8,128)(2,1)S(1)} %collective-permute-done.5.refs_4_), channel_id=1, source_target_pairs={{0,2},{1,3},{2,4},{3,5},{4,6},{5,7},{6,0},{7,1},{8,10},{9,11},{10,... | collective-permute-start | bytes 1105928 | tf_op jit(solution)/shard_map/ppermute | solution.py:124
  45.8 34.3 %collective-permute-start.8 = (bf16[240,768]{1,0:T(8,128)(2,1)S(1)}, bf16[240,768]{1,0:T(8,128)(2,1)S(1)}, u32[]{:S(2)}, u32[]{:S(2)}) collective-permute-start(bf16[240,768]{1,0:T(8,128)(2,1)S(1)} %collective-permute-done.5.refs_4_), channel_id=1, source_target_pairs={{0,1},{1,0},{2,3},{3,2},{4,5},{5,4},{6,7},{7,6},{8,9},{9,8},{10,11... | collective-permute-start | bytes 1105928 | tf_op jit(solution)/shard_map/ppermute | solution.py:129
  47.4 32.7 %collective-permute-start.11 = (bf16[192,768]{1,0:T(8,128)(2,1)}, bf16[192,768]{1,0:T(8,128)(2,1)}, u32[]{:S(2)}, u32[]{:S(2)}) collective-permute-start(bf16[192,768]{1,0:T(8,128)(2,1)} %copy-done.63), channel_id=1, source_target_pairs={{0,2},{1,3},{2,4},{3,5},{4,6},{5,7},{6,0},{7,1},{8,10},{9,11},{10,... | collective-permute-start | bytes 884744 | tf_op jit(solution)/shard_map/ppermute | solution.py:124
  47.9 32.2 %collective-permute-start.10 = (bf16[192,768]{1,0:T(8,128)(2,1)}, bf16[192,768]{1,0:T(8,128)(2,1)}, u32[]{:S(2)}, u32[]{:S(2)}) collective-permute-start(bf16[192,768]{1,0:T(8,128)(2,1)} %copy-done.63), channel_id=1, source_target_pairs={{0,1},{1,0},{2,3},{3,2},{4,5},{5,4},{6,7},{7,6},{8,9},{9,8},{10,11... | collective-permute-start | bytes 884744 | tf_op jit(solution)/shard_map/ppermute | solution.py:129
  104.2 19.8 %collective-permute-start.19 = (bf16[192,768]{1,0:T(8,128)(2,1)}, bf16[192,768]{1,0:T(8,128)(2,1)}, u32[]{:S(2)}, u32[]{:S(2)}) collective-permute-start(bf16[192,768]{1,0:T(8,128)(2,1)} %collective-permute-done.14.refs_6_), channel_id=1, source_target_pairs={{0,1},{1,0},{2,3},{3,2},{4,5},{5,4},{6,7},{7,6},{8,9},{9,8},{10,11... | collective-permute-start | bytes 884744 | tf_op jit(solution)/shard_map/ppermute | solution.py:129
  104.6 19.3 %collective-permute-start.20 = (bf16[192,768]{1,0:T(8,128)(2,1)}, bf16[192,768]{1,0:T(8,128)(2,1)S(1)}, u32[]{:S(2)}, u32[]{:S(2)}) collective-permute-start(bf16[192,768]{1,0:T(8,128)(2,1)} %collective-permute-done.11.refs_4_), channel_id=1, source_target_pairs={{0,16},{8,24},{16,0},{24,8},{1,17},{9,25},{17,1},{25,9},{2,18},{10... | collective-permute-start | bytes 884744 | tf_op jit(solution)/shard_map/ppermute | solution.py:132
  124.0 19.9 %collective-permute-start.23 = (bf16[192,768]{1,0:T(8,128)(2,1)}, bf16[192,768]{1,0:T(8,128)(2,1)S(1)}, u32[]{:S(2)}, u32[]{:S(2)}) collective-permute-start(bf16[192,768]{1,0:T(8,128)(2,1)} %collective-permute-done.14.refs_6_), channel_id=1, source_target_pairs={{0,16},{8,24},{16,0},{24,8},{1,17},{9,25},{17,1},{25,9},{2,18},{10... | collective-permute-start | bytes 884744 | tf_op jit(solution)/shard_map/ppermute | solution.py:132
  125.6 18.3 %collective-permute-start.24 = (bf16[192,768]{1,0:T(8,128)(2,1)}, bf16[192,768]{1,0:T(8,128)(2,1)}, u32[]{:S(2)}, u32[]{:S(2)}) collective-permute-start(bf16[192,768]{1,0:T(8,128)(2,1)} %collective-permute-done.19.refs_7_), channel_id=1, source_target_pairs={{0,16},{8,24},{16,0},{24,8},{1,17},{9,25},{17,1},{25,9},{2,18},{10... | collective-permute-start | bytes 884744 | tf_op jit(solution)/shard_map/ppermute | solution.py:132
  129.2 23.0 %collective-permute-start.25 = (bf16[8,96,768]{2,1,0:T(8,128)(2,1)}, bf16[8,96,768]{2,1,0:T(8,128)(2,1)}, u32[]{:S(2)}, u32[]{:S(2)}) collective-permute-start(bf16[8,96,768]{2,1,0:T(8,128)(2,1)} %get-tuple-element.146), channel_id=1, source_target_pairs={{0,8},{8,0},{16,24},{24,16},{1,9},{9,1},{17,25},{25,17},{2,10},{10... | collective-permute-start | bytes 3538952 | tf_op jit(solution)/shard_map/ppermute | solution.py:132
  129.2 23.0 %collective-permute-start.27 = (bf16[8,96,768]{2,1,0:T(8,128)(2,1)}, bf16[8,96,768]{2,1,0:T(8,128)(2,1)}, u32[]{:S(2)}, u32[]{:S(2)}) collective-permute-start(bf16[8,96,768]{2,1,0:T(8,128)(2,1)} %get-tuple-element.156), channel_id=1, source_target_pairs={{0,8},{8,0},{16,24},{24,16},{1,9},{9,1},{17,25},{25,17},{2,10},{10... | collective-permute-start | bytes 3538952 | tf_op jit(solution)/shard_map/ppermute | solution.py:132
  202.5 28.0 %collective-permute-start.33 = (bf16[8,96,768]{2,1,0:T(8,128)(2,1)S(1)}, bf16[8,96,768]{2,1,0:T(8,128)(2,1)S(1)}, u32[]{:S(2)}, u32[]{:S(2)}) collective-permute-start(bf16[8,96,768]{2,1,0:T(8,128)(2,1)S(1)} %fusion.10), channel_id=1, source_target_pairs={{0,16},{8,24},{16,0},{24,8},{1,17},{9,25},{17,1},{25,9},{2,18},{10... | collective-permute-start | bytes 3538952 | tf_op jit(solution)/shard_map/ppermute | solution.py:132
  233.3 27.5 %collective-permute-start.34 = (bf16[8,96,768]{2,1,0:T(8,128)(2,1)}, bf16[8,96,768]{2,1,0:T(8,128)(2,1)}, u32[]{:S(2)}, u32[]{:S(2)}) collective-permute-start(bf16[8,96,768]{2,1,0:T(8,128)(2,1)} %fusion.9), channel_id=1, source_target_pairs={{0,16},{8,24},{16,0},{24,8},{1,17},{9,25},{17,1},{25,9},{2,18},{10... | collective-permute-start | bytes 3538952 | tf_op jit(solution)/shard_map/ppermute | solution.py:132
  235.7 21.6 %collective-permute-start.35 = (bf16[4,96,768]{2,1,0:T(8,128)(2,1)}, bf16[4,96,768]{2,1,0:T(8,128)(2,1)}, u32[]{:S(2)}, u32[]{:S(2)}) collective-permute-start(bf16[4,96,768]{2,1,0:T(8,128)(2,1)} %dynamic-slice_bitcast_fusion.2), channel_id=1, source_target_pairs={{0,1},{1,0},{2,3},{3,2},{4,5},{5,4},{6,7},{7,6},{8,9},{9,8},{10,11... | collective-permute-start | bytes 1769480 | tf_op jit(solution)/shard_map/ppermute | solution.py:129
  298.8 24.4 %all-to-all-start.2 = ((bf16[8,2,64,384]{3,2,1,0:T(8,128)(2,1)}), bf16[8,2,64,384]{3,2,1,0:T(8,128)(2,1)}, u32[]{:S(2)}, u32[]{:S(2)}) async-start(bf16[8,2,64,384]{3,2,1,0:T(8,128)(2,1)} %fusion.42), calls=%async_computation.2 | async-start | bytes 1572864 | tf_op jit(solution)/shard_map/all_to_all | solution.py:682
  327.3 39.5 %collective-permute-start.44 = (bf16[4,232,768]{2,1,0:T(8,128)(2,1)}, bf16[4,232,768]{2,1,0:T(8,128)(2,1)}, u32[]{:S(2)}, u32[]{:S(2)}) collective-permute-start(bf16[4,232,768]{2,1,0:T(8,128)(2,1)} %dynamic-slice_bitcast_fusion), channel_id=1, source_target_pairs={{0,1},{1,0},{2,3},{3,2},{4,5},{5,4},{6,7},{7,6},{8,9},{9,8},{10,11... | collective-permute-start | bytes 4276232 | tf_op jit(solution)/shard_map/ppermute | solution.py:129
  329.7 40.0 %all-to-all-start.3 = ((bf16[8,2,64,384]{3,2,1,0:T(8,128)(2,1)}), bf16[8,2,64,384]{3,2,1,0:T(8,128)(2,1)}, u32[]{:S(2)}, u32[]{:S(2)}) async-start(bf16[8,2,64,384]{3,2,1,0:T(8,128)(2,1)} %slice.202), calls=%async_computation.3 | async-start | bytes 1572864 | tf_op jit(solution)/shard_map/all_to_all | solution.py:682
  334.0 35.7 %collective-permute-start.45 = (bf16[1024,384]{1,0:T(8,128)(2,1)}, bf16[1024,384]{1,0:T(8,128)(2,1)}, u32[]{:S(2)}, u32[]{:S(2)}) collective-permute-start(bf16[1024,384]{1,0:T(8,128)(2,1)} %bitcast.74), channel_id=1, source_target_pairs={{0,16},{8,24},{16,0},{24,8},{1,17},{9,25},{17,1},{25,9},{2,18},{10... | collective-permute-start | bytes 2359304 | tf_op jit(solution)/shard_map/ppermute | solution.py:132
  335.8 85.6 %collective-permute-start.51 = (s32[2048]{0:T(1024)S(1)}, s32[2048]{0:T(1024)S(1)}, u32[]{:S(2)}, u32[]{:S(2)}) collective-permute-start(s32[2048]{0:T(1024)S(1)} %eq.140), channel_id=1, source_target_pairs={{0,16},{8,24},{16,0},{24,8},{1,17},{9,25},{17,1},{25,9},{2,18},{10... | collective-permute-start | bytes 24584 | tf_op jit(solution)/shard_map/ppermute | solution.py:132
  369.7 51.0 %collective-permute-start.49 = (bf16[1024,384]{1,0:T(8,128)(2,1)}, bf16[1024,384]{1,0:T(8,128)(2,1)S(1)}, u32[]{:S(2)}, u32[]{:S(2)}) collective-permute-start(bf16[1024,384]{1,0:T(8,128)(2,1)} %bitcast.85), channel_id=1, source_target_pairs={{0,16},{8,24},{16,0},{24,8},{1,17},{9,25},{17,1},{25,9},{2,18},{10... | collective-permute-start | bytes 2359304 | tf_op jit(solution)/shard_map/ppermute | solution.py:132
  375.2 22.7 %collective-permute-start.48 = (bf16[328,768]{1,0:T(8,128)(2,1)S(1)}, bf16[328,768]{1,0:T(8,128)(2,1)S(1)}, u32[]{:S(2)}, u32[]{:S(2)}) collective-permute-start(bf16[328,768]{1,0:T(8,128)(2,1)S(1)} %get-tuple-element.250), channel_id=1, source_target_pairs={{0,6},{1,7},{2,0},{3,1},{4,2},{5,3},{6,4},{7,5},{8,14},{9,15},{10,... | collective-permute-start | bytes 1511432 | tf_op jit(solution)/shard_map/ppermute | solution.py:124
  379.3 40.1 %collective-permute-start.47 = (bf16[328,768]{1,0:T(8,128)(2,1)S(1)}, bf16[328,768]{1,0:T(8,128)(2,1)S(1)}, u32[]{:S(2)}, u32[]{:S(2)}) collective-permute-start(bf16[328,768]{1,0:T(8,128)(2,1)S(1)} %get-tuple-element.251), channel_id=1, source_target_pairs={{0,4},{1,5},{2,6},{3,7},{4,0},{5,1},{6,2},{7,3},{8,12},{9,13},{10,... | collective-permute-start | bytes 1511432 | tf_op jit(solution)/shard_map/ppermute | solution.py:124
  (111 other events, 910.5 us)

commit v3 on v2

--- a/solution.py
+++ b/solution.py
@@ -143,6 +143,10 @@
         return jnp.stack([(a - k + A) % A * B + (b - m + B) % B for k in range(A) for m in range(B)])
 
     def fold_b(self, total, axis):
+        sent, kept = self.last_b(total, axis)
+        return add(self.step_b(sent), kept)
+
+    def last_b(self, total, axis):
         B = self.B
         here = self.place()[1]
 
@@ -150,17 +154,16 @@
             return pick(total, index % B, axis + 1)
 
         held = block(here - 1 + B)
-        for s in range(1, B):
+        for s in range(1, B - 1):
             held = add(self.step_b(held), block(here - 1 - s + 2 * B))
-        return held
-
-    def fold_a(self, total, axis):
-        A = self.A
+        return held, block(here)
+
+    def cut_a(self, total, axis):
         here = self.place()[0]
-        terms = [pick(total, here, axis)]
-        for far in range(1, A):
-            terms.append(self.step_a(pick(total, (here + far) % A, axis), far))
-        return add(*terms)
+        return [pick(total, (here + far) % self.A, axis) for far in range(self.A)]
+
+    def sent_a(self, terms):
+        return [self.step_a(terms[far], far) for far in range(1, self.A)]
 
     def split(self, total, axis):
         return total.reshape(total.shape[:axis] + (self.A, self.B) + total.shape[axis + 1 :])
@@ -305,19 +308,6 @@
         query_sum_ref[:, lanes] = jnp.sum(query_grad.astype(jnp.float32), axis=0, keepdims=True)
 
 
-def attend_back_call(length, query, key, value, grad):
-    like = jax.ShapeDtypeStruct(query.shape, jnp.bfloat16)
-    line = jax.ShapeDtypeStruct((1, query.shape[1]), jnp.float32)
-    return pl.pallas_call(
-        attend_back_kernel,
-        out_shape=(like, like, like, line, line),
-        in_specs=[SMEM] + whole(4),
-        out_specs=tuple(whole(5)),
-        cost_estimate=cost(3),
-        name="attend_back",
-    )(length, query, key, value, grad)
-
-
 def hidden_kernel(rows_ref, shift_ref, *refs):
     inner_refs, outer_refs, active_refs, slope_refs = (refs[4 * i : 4 * i + 4] for i in range(4))
     branch_ref = refs[16]
@@ -349,6 +339,36 @@
         name="hidden",
     )(rows, shift, *inner, *outer)
     return out[:4], out[4:8], out[8]
+
+
+def normed_back_kernel(first_ref, hat_ref, inverse_ref, scale_ref, *refs):
+    grads, weights, (out_ref, gain_ref, bias_ref) = refs[:3], refs[3:6], refs[6:]
+    upstream = first_ref[...]
+    for grad, weight in zip(grads, weights):
+        upstream = upstream + dot(grad[...], weight[...], ((1,), (1,)))
+    hat = hat_ref[...]
+    gain_ref[...] = jnp.sum(upstream * hat, axis=0, keepdims=True)
+    bias_ref[...] = jnp.sum(upstream, axis=0, keepdims=True)
+    out_ref[...] = normalize_back(upstream, hat, inverse_ref[...], scale_ref[...]).astype(jnp.bfloat16)
+
+
+def front_back_kernel(*refs):
+    attention, norm, weights, outs = refs[:5], refs[5:9], refs[9:12], refs[12:]
+    attend_back_kernel(*attention, *outs[:5])
+    normed_back_kernel(*norm, *outs[:3], *weights, *outs[5:])
+
+
+def front_back_call(length, query, key, value, grad, first, hat, inverse, scale, weights):
+    like = jax.ShapeDtypeStruct(query.shape, jnp.bfloat16)
+    line = jax.ShapeDtypeStruct((1, query.shape[1]), jnp.float32)
+    return pl.pallas_call(
+        front_back_kernel,
+        out_shape=(like, like, like, line, line, like, line, line),
+        in_specs=[SMEM] + whole(11),
+        out_specs=tuple(whole(8)),
+        cost_estimate=cost(1),
+        name="front_back",
+    )(length, query, key, value, grad, first, hat, inverse, scale.reshape(1, -1), *weights)
 
 
 def widen_kernel(core_ref, here_ref, there_ref, out_ref):
@@ -574,9 +594,10 @@
         for i in range(4)
     ]
     inner_grad, outer_cross = tie(inner_grad, outer_cross)
-    outer_sent, inner_grad = tie(add(outer_terms[2], outer_cross[0]), inner_grad)
-    outer_across = links.swap(outer_sent, 2)
-    outer_near = add(outer_terms[0], outer_cross[1])
+    outer_pair = jnp.concatenate(
+        [add(outer_terms[0], outer_cross[1]), add(outer_terms[2], outer_cross[0])], axis=1
+    )
+    outer_pair, inner_grad = tie(links.split(outer_pair, 0), inner_grad)
     inner_bias_gradient = [jnp.sum(item.astype(jnp.float32), axis=0) for item in inner_grad]
     inner_terms = [None] * 4
     for i in (3, 1, 2, 0):
@@ -584,14 +605,8 @@
         inner_terms[i] = inner_terms[i].reshape(owners, rows, width)
     inner_cross = [links.swap(inner_terms[i], 1) for i in (3, 1)]
     middle_grad = second + sum(times_transposed(inner_grad[i], inner_matrix[i]) for i in range(4))
-    middle_grad, inner_cross, outer_across = tie(middle_grad, inner_cross, outer_across)
-    inner_across_sent, outer_whole, middle_grad = tie(
-        add(inner_terms[2], inner_cross[0]),
-        links.split(add(outer_near, outer_across), 0),
-        middle_grad,
-    )
-    inner_across = links.swap(inner_across_sent, 2)
-    outer_half = links.fold_b(outer_whole, 0)
+    middle_grad, inner_cross = tie(middle_grad, inner_cross)
+    inner_sent, middle_grad = tie(add(inner_terms[2], inner_cross[0]), middle_grad)
     inner_near = add(inner_terms[0], inner_cross[1])
     middle_gain_gradient = jnp.sum(middle_grad * hat_middle, axis=0)
     middle_bias_gradient = jnp.sum(middle_grad, axis=0)
@@ -599,58 +614,45 @@
     attended_grad = first.astype(jnp.bfloat16)
     output_bias_gradient = jnp.sum(attended_grad.astype(jnp.float32), axis=0)
     context_grad = times_transposed(attended_grad, output_matrix).astype(jnp.bfloat16)
-    query_low_grad, key_low_grad, value_low_grad, query_bias_gradient, value_bias_gradient = (
-        attend_back_call(lengths, query_low, key_low, value_low, context_grad)
-    )
-    query_low_grad, key_low_grad, value_low_grad, inner_across, outer_half = tie(
-        query_low_grad, key_low_grad, value_low_grad, inner_across, outer_half
-    )
-    outer_share = links.fold_a(outer_half, 0)
-    inner_half = links.fold_b(links.split(add(inner_near, inner_across), 0), 0)
+    outer_sent, outer_kept = links.last_b(outer_pair, 0)
+    context_grad, inner_sent, outer_sent = tie(context_grad, inner_sent, outer_sent)
+    inner_across = links.swap(inner_sent, 2)
+    outer_held = links.step_b(outer_sent)
+    back = front_back_call(
+        lengths, query_low, key_low, value_low, context_grad, first, hat_embed, inv_embed,
+        embed_scale, (query_matrix, key_matrix, value_matrix),
+    )
+    back, inner_across, outer_held = tie(back, inner_across, outer_held)
+    (
+        query_low_grad, key_low_grad, value_low_grad, query_bias_gradient, value_bias_gradient,
+        embedded_grad, embed_gain_gradient, embed_bias_gradient,
+    ) = back
     own_left = jnp.where(core == 0, normed_low, context)
     sent_left = jnp.where(core == 0, context, normed_low)
     square_sent = [
         local_terms(normed_low, jnp.where(core == 0, value_low_grad, query_low_grad)),
         local_terms(sent_left, jnp.where(core == 0, attended_grad, key_low_grad)),
     ]
-    square_cross = [links.swap(item, 1) for item in square_sent]
     square_own = [
         local_terms(normed_low, jnp.where(core == 0, query_low_grad, value_low_grad)),
         local_terms(own_left, jnp.where(core == 0, key_low_grad, attended_grad)),
     ]
-    normed_grad = (
-        first
-        + times_transposed(query_low_grad, query_matrix)
-        + times_transposed(key_low_grad, key_matrix)
-        + times_transposed(value_low_grad, value_matrix)
-    )
-    embed_gain_gradient = jnp.sum(normed_grad * hat_embed, axis=0)
-    embed_bias_gradient = jnp.sum(normed_grad, axis=0)
-    summed_grad = normalize_back(normed_grad, hat_embed, inv_embed, embed_scale)
-    embedded_grad = summed_grad.astype(jnp.bfloat16)
-    embedded_grad, outer_share, inner_half, square_cross = tie(
-        embedded_grad, outer_share, inner_half, square_cross
-    )
-
+    square_cross = [links.swap(item, 1) for item in square_sent]
+    outer_half = add(outer_held, outer_kept)
+    outer_across = links.swap(outer_half[:, rows:], 2)
+    inner_half = links.fold_b(links.split(add(inner_near, inner_across), 0), 0)
     wide = width // 2
-    features = [embedded_grad[:, :wide], embedded_grad[:, wide:]]
-
-    def rows_of(features):
-        return jnp.einsum(
-            "ts,td->sd", route, features, preferred_element_type=jnp.float32
-        ).astype(jnp.bfloat16)
-
-    kept = rows_of(jnp.where(core == 0, features[0], features[1]))
-    given = links.swap(rows_of(jnp.where(core == 0, features[1], features[0])), 1)
-    leaving = jnp.stack(
-        [item.reshape(owners, cap, wide) for item in ordered(kept, given)], axis=1
-    )
-    known = jnp.stack(
-        [item.reshape(owners, cap) for item in ordered(held_ids, links.swap(held_ids, 1))], axis=1
-    )
+    leaving = jnp.einsum("ts,td->sd", route, embedded_grad, preferred_element_type=jnp.float32)
+    leaving = leaving.astype(jnp.bfloat16).reshape(owners, cap, width)
     parts = 2
     cut = cap // parts
-    known = known.reshape(owners, 2, parts, cut).transpose(2, 0, 1, 3).reshape(-1)
+    known = jnp.stack(
+        [
+            item.reshape(owners, parts, cut).transpose(1, 0, 2)
+            for item in (held_ids, links.swap(held_ids, 1))
+        ],
+        axis=1,
+    ).reshape(-1)
     known_sets = [known]
     bit = 2
     while bit < groups:
@@ -678,11 +680,13 @@
         bit *= 2
 
     def exchange(part):
-        piece = leaving[:, :, part * cut : (part + 1) * cut]
+        piece = leaving[:, part * cut : (part + 1) * cut]
         return lax.all_to_all(piece, "vocab", 0, 0, tiled=True)
 
-    def beyond(piece):
-        items = [piece]
+    def beyond(landed):
+        landed = landed.reshape(-1, width)
+        mine, theirs = ordered(landed[:, :wide], landed[:, wide:])
+        items = [jnp.concatenate([mine, links.swap(theirs, 1)])]
         for bit in bits:
             items = items + [links.swap(item, bit) for item in items]
         return items
@@ -691,7 +695,6 @@
         return matmul((table_ids[:, None] == known[None, :]).astype(jnp.bfloat16), pieces)
 
     table_ids = lax.iota(jnp.int32, table_rows)
-    landed, late_cross, leaving = tie(exchange(0).reshape(-1, wide), late_cross, leaving)
     late_whole = jnp.concatenate(
         [
             add(square_own[0], square_cross[0]),
@@ -700,27 +703,44 @@
         ],
         axis=1,
     )
-    late_half = links.fold_b(links.split(late_whole, 0), 0)
+    landed, late_whole, leaving, outer_across, inner_half = tie(
+        exchange(0), links.split(late_whole, 0), leaving, outer_across, inner_half
+    )
+    late_half = links.fold_b(late_whole, 0)
     first_sets = beyond(landed)
-    landed, late_half, first_sets = tie(exchange(1).reshape(-1, wide), late_half, first_sets)
-    share = links.fold_a(jnp.concatenate([inner_half, late_half], axis=1), 0)
+    outer_cut = links.cut_a(add(outer_half[:, :rows], outer_across), 0)
+    outer_arrived = links.sent_a(outer_cut)
+    landed, first_sets, outer_arrived = tie(exchange(1), first_sets, outer_arrived)
+    inner_cut = links.cut_a(inner_half, 0)
+    inner_arrived = links.sent_a(inner_cut)
     second_sets = beyond(landed)
     table_sum = [table_term(jnp.concatenate([first_sets[0], second_sets[0]]), known_sets[0])]
-    share, second_sets, table_sum = tie(share, second_sets, table_sum)
-    share = links.far(jnp.concatenate([outer_share, share]), 4)
-    share_beyond = links.swap(share, 2)
+    table_sum, late_half, second_sets, inner_arrived = tie(
+        table_sum, late_half, second_sets, inner_arrived
+    )
+    late_cut = links.cut_a(late_half, 0)
+    late_arrived = links.sent_a(late_cut)
+    hidden_share = jnp.concatenate(
+        [add(outer_cut[0], *outer_arrived), add(inner_cut[0], *inner_arrived)]
+    )
+    hidden_share = links.far(hidden_share, 4)
+    hidden_beyond = links.swap(hidden_share, 2)
     for i in range(1, len(known_sets)):
         pieces = jnp.concatenate([first_sets[i], second_sets[i]])
         table_sum.append(table_term(pieces, known_sets[i]))
     while len(table_sum) > 1:
         table_sum = [a + b for a, b in zip(table_sum[::2], table_sum[1::2])]
-    table_half, share_beyond = tie(table_sum[0].astype(jnp.bfloat16), share_beyond)
-    late_share = add(share[2 * rows :], share_beyond[2 * rows :])
-    share_core = jnp.concatenate([share[: 2 * rows], share_beyond[: 2 * rows], late_share])
-    table_other, share_other = links.swap(table_half, 1), links.swap(share_core, 1)
-    table_other, share_other = tie(table_other, share_other)
+    table_half, hidden_beyond, late_arrived = tie(
+        table_sum[0].astype(jnp.bfloat16), hidden_beyond, late_arrived
+    )
+    late_share = add(late_cut[0], *late_arrived)
+    hidden_core = jnp.concatenate([hidden_share, hidden_beyond])
+    hidden_other = links.swap(hidden_core, 1)
+    table_other = links.swap(table_half, 1)
+    late_share = links.far(late_share, 2)
+    late_other = links.swap(late_share, 1)
     table_gradient = widen_call(core, table_half, table_other)
-    low_share, high_share = ordered(share_core[4 * rows :], share_other[4 * rows :])
+    low_share, high_share = ordered(late_share, late_other)
     first_share, second_share = low_share[:rows], low_share[rows : 2 * rows]
     third_share, fourth_share = high_share[:rows], high_share[rows : 2 * rows]
     place_end = 2 * rows + place_part
@@ -737,7 +757,7 @@
     inner_bias_gradient = vector_share[10:14].reshape(4 * rows)
 
     def quad(start):
-        own, beside = share_core[start : start + 3 * rows], share_other[start : start + 3 * rows]
+        own, beside = hidden_core[start : start + 3 * rows], hidden_other[start : start + 3 * rows]
         items = [own[:rows], beside[:rows], own[2 * rows :], beside[2 * rows :]]
         return jnp.stack(items)[jnp.stack(blocks)]
 

time: 472 us -> 447 us (0.947)
  waiting for transfers between devices: 151 us -> 113 us
  other arithmetic: 48.1 us -> 58.3 us
  matrix products: 70.8 us -> 64.1 us
    ppermute x11, waiting for transfers between devices: 29.8 us -> 7.82 us  [step_b(): return lax.ppermute(piece, 'vocab', pairs)]
    unnamed x154 -> x152, local copies, waits for them, and re-layouts: 18.2 us -> 10.8 us
    dot_general x12 -> x9, matrix products: 20.8 us -> 14.8 us  [times_transposed(): jnp.einsum('tj,ij->ti', left, right, preferred_element_type=jnp.float32)]
    ppermute x32 -> x35, waiting for transfers between devices: 37.7 us -> 31.9 us  [swap(): return lax.ppermute(piece, 'dp', [(i, i ^ bit) for i in range(self.groups)])]
    ppermute x12 -> x15, waiting for transfers between devices: 74.4 us -> 68.7 us  [step_a(): return lax.ppermute(piece, 'vocab', pairs)]
    all_to_all x2, starting transfers between devices: 8.42 us -> 13.6 us  [exchange(): return lax.all_to_all(piece, 'vocab', 0, 0, tiled=True)]
    convert_element_type x13 -> x15, other arithmetic: 14.2 us -> 19.2 us  [add(): sum((term.astype(jnp.float32) for term in terms)).astype(jnp.bfloat16)]
    convert_element_type x3, local copies, waits for them, and re-layouts: 4.41 us -> 9.16 us  [wider(): return share.astype(jnp.float32)]
  transfers between devices with their start and end apart: 59 -> 65, of which waited for: 18 -> 16; matrix products, arithmetic and copies ran while one was open for 23% -> 29% of each run, Pallas kernels for 8% -> 9%
where the time goes in v3:
time: 447 us; the launch traced here: 440 us
  waiting for transfers between devices  113 us (25%)
  starting transfers between devices  79.8 us (18%)
  Pallas kernels  68.1 us (15%)
  matrix products  64.1 us (14%)
  other arithmetic  58.3 us (13%)
  local copies, waits for them, and re-layouts  53.2 us (12%)
    ppermute x15, waiting for transfers between devices, step_a(): return lax.ppermute(piece, 'vocab', pairs)  68.7 us
    ppermute x35, waiting for transfers between devices, swap(): return lax.ppermute(piece, 'dp', [(i, i ^ bit) for i in range(self.groups)])  31.9 us
    dot_general x8, matrix products, matmul(): return jnp.dot(left, right, preferred_element_type=jnp.float32)  31.8 us
    ppermute x15, starting transfers between devices, step_a(): return lax.ppermute(piece, 'vocab', pairs)  26 us
    pallas_call x1, Pallas kernels, front_back_call(): pl.pallas_call(front_back_kernel, out_shape=(like, like, like, line, line...  21.4 us
    pallas_call x1, Pallas kernels, hidden_call(): pl.pallas_call(hidden_kernel, out_shape=(like,) * 8 + (jax.ShapeDtypeStru...  19.3 us
    convert_element_type x15, other arithmetic, add(): sum((term.astype(jnp.float32) for term in terms)).astype(jnp.bfloat16)  19.2 us
    ppermute x35, starting transfers between devices, swap(): return lax.ppermute(piece, 'dp', [(i, i ^ bit) for i in range(self.groups)])  18.9 us
  transfers between devices with their start and end apart: 65, of which 16 were waited for; matrix products, arithmetic and copies ran while one was open for 29% of the time, Pallas kernels for 9%

profile of v3, /device:TPU:0, one launch (start us, length us, event | category | flops | bytes accessed | tf_op | source)
XLA Modules:
  0.0 440.0 jit_solution(5832183735214413151)
XLA Ops:
  10.2 3.9 all-to-all-start
  21.7 7.9 %gather_fusion = bf16[1024,768]{1,0:T(8,128)(2,1)S(1)} fusion(bf16[3840,768]{1,0:T(8,128)(2,1)} %param.24, s32[1024]{0:T(1024)S(1)} %broadcast_clamp_fusion), kind=kCustom, calls=%fused_computation | custom fusion | bytes 3149824 | tf_op jit(solution)/shard_map/jit(_take)/gather | solution.py:483
  35.2 5.1 %all-to-all-start.1 = ((bf16[8,128,768]{2,1,0:T(8,128)(2,1)}), bf16[8,128,768]{2,1,0:T(8,128)(2,1)}, u32[]{:S(2)}, u32[]{:S(2)}) async-start(bf16[8,128,768]{2,1,0:T(8,128)(2,1)} %bitcast.21), calls=%async_computation.1 | async-start | bytes 3145728 | tf_op jit(solution)/shard_map/all_to_all | solution.py:509
  50.0 31.8 %collective-permute-done.11.refs_4_ = bf16[192,768]{1,0:T(8,128)(2,1)} collective-permute-done((bf16[192,768]{1,0:T(8,128)(2,1)S(1)}, bf16[192,768]{1,0:T(8,128)(2,1)}, u32[]{:S(2)}, u32[]{:S(2)}) %collective-permute-start.11) | collective-permute-done | bytes 294944 | tf_op jit(solution)/shard_map/ppermute | solution.py:124
  84.7 6.5 %collective-permute-start.14 = (bf16[192,768]{1,0:T(8,128)(2,1)}, bf16[192,768]{1,0:T(8,128)(2,1)}, u32[]{:S(2)}, u32[]{:S(2)}) collective-permute-start(bf16[192,768]{1,0:T(8,128)(2,1)} %collective-permute-done.11.refs_4_), channel_id=1, source_target_pairs={{0,2},{1,3},{2,4},{3,5},{4,6},{5,7},{6,0},{7,1},{8,10},{9,11},{10,... | collective-permute-start | bytes 884744 | tf_op jit(solution)/shard_map/ppermute | solution.py:124
  93.5 3.6 collective-permute-done.14.refs_6_
  100.0 3.5 arrange.3
  134.8 9.2 %attend.1 = bf16[512,768]{1,0:T(8,128)(2,1)} custom-call(s32[1]{0:T(128)S(6)} %copy.132.length_ref.refs_0_, bf16[512,768]{1,0:T(8,128)(2,1)} %add_convert_fusion.4.query_ref.refs_1_, bf16[512,768]{1,0:T(8,128)(2,1)} %convolution_convert_fusion.13.key_ref.refs_2_, bf16[512,768]{1,0:T(8,128)(2,1)} %add_convert_fusion.3.value_ref.refs_3_), custom_call_target="tpu_custom_call" | custom-call | bytes 12000000 | tf_op jit(solution)/shard_map/attend/pallas_call | solution.py:262
  153.5 19.3 %hidden.1 = (bf16[512,768]{1,0:T(8,128)(2,1)}, bf16[512,768]{1,0:T(8,128)(2,1)}, bf16[512,768]{1,0:T(8,128)(2,1)}, bf16[512,768]{1,0:T(8,128)(2,1)}, bf16[512,76...) custom-call(bf16[512,768]{1,0:T(8,128)(2,1)} %fusion.31.rows_ref, ...), custom_call_target="tpu_custom_call" | custom-call | bytes 24000000 | tf_op jit(solution)/shard_map/hidden/pallas_call | solution.py:333
  220.2 21.4 %front_back.1 = (bf16[512,768]{1,0:T(8,128)(2,1)}, bf16[512,768]{1,0:T(8,128)(2,1)}, bf16[512,768]{1,0:T(8,128)(2,1)}, f32[1,768]{1,0:T(1,128)}, f32[1,768]{1,0:...) custom-call(s32[1]{0:T(128)S(6)} %copy.132.length_ref.refs_0_, ...), custom_call_target="tpu_custom_call" | custom-call | bytes 3000000 | tf_op jit(solution)/shard_map/front_back/pallas_call | solution.py:364
  258.6 9.4 %all-to-all-start.2 = ((bf16[8,64,768]{2,1,0:T(8,128)(2,1)}), bf16[8,64,768]{2,1,0:T(8,128)(2,1)}, u32[]{:S(2)}, u32[]{:S(2)}) async-start(bf16[8,64,768]{2,1,0:T(8,128)(2,1)} %slice.239), calls=%async_computation.2 | async-start | bytes 1572864 | tf_op jit(solution)/shard_map/all_to_all | solution.py:684
  277.5 7.8 %collective-permute-done.39 = bf16[4,96,768]{2,1,0:T(8,128)(2,1)} collective-permute-done((bf16[4,96,768]{2,1,0:T(8,128)(2,1)S(1)}, bf16[4,96,768]{2,1,0:T(8,128)(2,1)}, u32[]{:S(2)}, u32[]{:S(2)}) %collective-permute-start.39) | collective-permute-done | bytes 589856 | tf_op jit(solution)/shard_map/ppermute | solution.py:132
  285.3 4.3 all-to-all-done.2
  291.7 4.2 all-to-all-start.3
  314.7 14.5 %collective-permute-done.44 = bf16[96,768]{1,0:T(8,128)(2,1)} collective-permute-done((bf16[96,768]{1,0:T(8,128)(2,1)}, bf16[96,768]{1,0:T(8,128)(2,1)}, u32[]{:S(2)}, u32[]{:S(2)}) %collective-permute-start.44) | collective-permute-done | bytes 147488 | tf_op jit(solution)/shard_map/ppermute | solution.py:124
  332.0 5.6 %collective-permute-done.47 = bf16[4,232,768]{2,1,0:T(8,128)(2,1)} collective-permute-done((bf16[4,232,768]{2,1,0:T(8,128)(2,1)}, bf16[4,232,768]{2,1,0:T(8,128)(2,1)}, u32[]{:S(2)}, u32[]{:S(2)}) %collective-permute-start.47) | collective-permute-done | bytes 1425440 | tf_op jit(solution)/shard_map/ppermute | solution.py:129
  341.8 9.7 %fusion = f32[3840,384]{1,0:T(8,128)S(1)} fusion(s32[2048]{0:T(1024)S(1)} %eq.144, bf16[512,384]{1,0:T(8,128)(2,1)S(1)} %collective-permute-done.46, bf16[512,384]{1,0:T(8,128)(2,1)S(1)} %get-tuple-element.274, bf16[1024,384]{1,0:T(8,128)(2,1)} %pad_maximum_fusion.2), kind=kOutput, calls=%fused_computation.6 | convolution fusion | flops 6052380672 | bytes 7479296 | tf_op jit(solution)/shard_map/dot_general | solution.py:41
  351.5 8.8 %collective-permute-done.48 = bf16[1024,384]{1,0:T(8,128)(2,1)S(1)} collective-permute-done((bf16[1024,384]{1,0:T(8,128)(2,1)S(1)}, bf16[1024,384]{1,0:T(8,128)(2,1)S(1)}, u32[]{:S(2)}, u32[]{:S(2)}) %collective-permute-start.48) | collective-permute-done | bytes 786464 | tf_op jit(solution)/shard_map/ppermute | solution.py:132
  367.2 9.7 %fusion.1 = f32[3840,384]{1,0:T(8,128)S(1)} fusion(s32[2048]{0:T(1024)S(1)} %collective-permute-done.52, bf16[1024,384]{1,0:T(8,128)(2,1)S(1)} %collective-permute-done.48, bf16[1024,384]{1,0:T(8,128)(2,1)} %collective-permute-done.42), kind=kOutput, calls=%fused_computation.7 | convolution fusion | flops 6050807808 | bytes 7479296 | tf_op jit(solution)/shard_map/dot_general | solution.py:41
  377.7 17.3 %collective-permute-done.55 = bf16[232,768]{1,0:T(8,128)(2,1)S(1)} collective-permute-done((bf16[232,768]{1,0:T(8,128)(2,1)S(1)}, bf16[232,768]{1,0:T(8,128)(2,1)S(1)}, u32[]{:S(2)}, u32[]{:S(2)}) %collective-permute-start.55) | collective-permute-done | bytes 356384 | tf_op jit(solution)/shard_map/ppermute | solution.py:124
  397.8 8.2 %collective-permute-done.58 = bf16[232,768]{1,0:T(8,128)(2,1)S(1)} collective-permute-done((bf16[232,768]{1,0:T(8,128)(2,1)S(1)}, bf16[232,768]{1,0:T(8,128)(2,1)S(1)}, u32[]{:S(2)}, u32[]{:S(2)}) %collective-permute-start.58) | collective-permute-done | bytes 356384 | tf_op jit(solution)/shard_map/ppermute | solution.py:132
  415.7 3.6 copy.126
  419.3 3.7 reshape.665
  431.1 8.5 %widen.1 = f32[3840,768]{1,0:T(8,128)} custom-call(s32[1]{0:T(128)} %bitcast.48.core_ref, bf16[3840,384]{1,0:T(8,128)(2,1)} %copy-done.3, bf16[3840,384]{1,0:T(8,128)(2,1)} %collective-permute-done.57.there_ref), custom_call_target="tpu_custom_call" | custom-call | bytes 15000000 | tf_op jit(solution)/shard_map/widen/pallas_call | solution.py:391
  (458 shorter events, 209.6 us)
Async XLA Ops:
  4.3 26.7 %collective-permute-start.1 = (bf16[240,768]{1,0:T(8,128)(2,1)S(1)}, bf16[240,768]{1,0:T(8,128)(2,1)S(1)}, u32[]{:S(2)}, u32[]{:S(2)}) collective-permute-start(bf16[240,768]{1,0:T(8,128)(2,1)S(1)} %pad_maximum_fusion.7.refs_0_), channel_id=1, source_target_pairs={{0,2},{1,3},{2,4},{3,5},{4,6},{5,7},{6,0},{7,1},{8,10},{9,11},{10,... | collective-permute-start | bytes 1105928 | tf_op jit(solution)/shard_map/ppermute | solution.py:124
  7.4 24.4 %collective-permute-start = (bf16[240,768]{1,0:T(8,128)(2,1)S(1)}, bf16[240,768]{1,0:T(8,128)(2,1)}, u32[]{:S(2)}, u32[]{:S(2)}) collective-permute-start(bf16[240,768]{1,0:T(8,128)(2,1)S(1)} %pad_maximum_fusion.7.refs_0_), channel_id=1, source_target_pairs={{0,1},{1,0},{2,3},{3,2},{4,5},{5,4},{6,7},{7,6},{8,9},{9,8},{10,11... | collective-permute-start | bytes 1105928 | tf_op jit(solution)/shard_map/ppermute | solution.py:129
  35.2 82.6 %all-to-all-start.1 = ((bf16[8,128,768]{2,1,0:T(8,128)(2,1)}), bf16[8,128,768]{2,1,0:T(8,128)(2,1)}, u32[]{:S(2)}, u32[]{:S(2)}) async-start(bf16[8,128,768]{2,1,0:T(8,128)(2,1)} %bitcast.21), calls=%async_computation.1 | async-start | bytes 3145728 | tf_op jit(solution)/shard_map/all_to_all | solution.py:509
  46.1 35.7 %collective-permute-start.9 = (bf16[240,768]{1,0:T(8,128)(2,1)S(1)}, bf16[240,768]{1,0:T(8,128)(2,1)S(1)}, u32[]{:S(2)}, u32[]{:S(2)}) collective-permute-start(bf16[240,768]{1,0:T(8,128)(2,1)S(1)} %collective-permute-done.5.refs_4_), channel_id=1, source_target_pairs={{0,2},{1,3},{2,4},{3,5},{4,6},{5,7},{6,0},{7,1},{8,10},{9,11},{10,... | collective-permute-start | bytes 1105928 | tf_op jit(solution)/shard_map/ppermute | solution.py:124
  47.6 34.2 %collective-permute-start.8 = (bf16[240,768]{1,0:T(8,128)(2,1)S(1)}, bf16[240,768]{1,0:T(8,128)(2,1)S(1)}, u32[]{:S(2)}, u32[]{:S(2)}) collective-permute-start(bf16[240,768]{1,0:T(8,128)(2,1)S(1)} %collective-permute-done.5.refs_4_), channel_id=1, source_target_pairs={{0,1},{1,0},{2,3},{3,2},{4,5},{5,4},{6,7},{7,6},{8,9},{9,8},{10,11... | collective-permute-start | bytes 1105928 | tf_op jit(solution)/shard_map/ppermute | solution.py:129
  49.0 32.7 %collective-permute-start.11 = (bf16[192,768]{1,0:T(8,128)(2,1)S(1)}, bf16[192,768]{1,0:T(8,128)(2,1)}, u32[]{:S(2)}, u32[]{:S(2)}) collective-permute-start(bf16[192,768]{1,0:T(8,128)(2,1)S(1)} %collective-permute-done.3.refs_2_), channel_id=1, source_target_pairs={{0,2},{1,3},{2,4},{3,5},{4,6},{5,7},{6,0},{7,1},{8,10},{9,11},{10,... | collective-permute-start | bytes 884744 | tf_op jit(solution)/shard_map/ppermute | solution.py:124
  49.6 32.2 %collective-permute-start.10 = (bf16[192,768]{1,0:T(8,128)(2,1)S(1)}, bf16[192,768]{1,0:T(8,128)(2,1)}, u32[]{:S(2)}, u32[]{:S(2)}) collective-permute-start(bf16[192,768]{1,0:T(8,128)(2,1)S(1)} %collective-permute-done.3.refs_2_), channel_id=1, source_target_pairs={{0,1},{1,0},{2,3},{3,2},{4,5},{5,4},{6,7},{7,6},{8,9},{9,8},{10,11... | collective-permute-start | bytes 884744 | tf_op jit(solution)/shard_map/ppermute | solution.py:129
  129.6 23.8 %collective-permute-start.25 = (bf16[8,96,768]{2,1,0:T(8,128)(2,1)}, bf16[8,96,768]{2,1,0:T(8,128)(2,1)}, u32[]{:S(2)}, u32[]{:S(2)}) collective-permute-start(bf16[8,96,768]{2,1,0:T(8,128)(2,1)} %get-tuple-element.158), channel_id=1, source_target_pairs={{0,8},{8,0},{16,24},{24,16},{1,9},{9,1},{17,25},{25,17},{2,10},{10... | collective-permute-start | bytes 3538952 | tf_op jit(solution)/shard_map/ppermute | solution.py:132
  129.6 23.8 %collective-permute-start.27 = (bf16[8,96,768]{2,1,0:T(8,128)(2,1)}, bf16[8,96,768]{2,1,0:T(8,128)(2,1)}, u32[]{:S(2)}, u32[]{:S(2)}) collective-permute-start(bf16[8,96,768]{2,1,0:T(8,128)(2,1)} %get-tuple-element.168), channel_id=1, source_target_pairs={{0,8},{8,0},{16,24},{24,16},{1,9},{9,1},{17,25},{25,17},{2,10},{10... | collective-permute-start | bytes 3538952 | tf_op jit(solution)/shard_map/ppermute | solution.py:132
  210.9 30.7 %collective-permute-start.34 = (bf16[8,96,768]{2,1,0:T(8,128)(2,1)}, bf16[8,96,768]{2,1,0:T(8,128)(2,1)}, u32[]{:S(2)}, u32[]{:S(2)}) collective-permute-start(bf16[8,96,768]{2,1,0:T(8,128)(2,1)} %fusion.9), channel_id=1, source_target_pairs={{0,16},{8,24},{16,0},{24,8},{1,17},{9,25},{17,1},{25,9},{2,18},{10... | collective-permute-start | bytes 3538952 | tf_op jit(solution)/shard_map/ppermute | solution.py:132
  212.4 29.2 %collective-permute-start.35 = (bf16[4,192,768]{2,1,0:T(8,128)(2,1)}, bf16[4,192,768]{2,1,0:T(8,128)(2,1)}, u32[]{:S(2)}, u32[]{:S(2)}) collective-permute-start(bf16[4,192,768]{2,1,0:T(8,128)(2,1)} %dynamic-slice_bitcast_fusion.1), channel_id=1, source_target_pairs={{0,1},{1,0},{2,3},{3,2},{4,5},{5,4},{6,7},{7,6},{8,9},{9,8},{10,11... | collective-permute-start | bytes 3538952 | tf_op jit(solution)/shard_map/ppermute | solution.py:129
  251.1 22.9 %collective-permute-start.37 = (bf16[8,96,768]{2,1,0:T(8,128)(2,1)}, bf16[8,96,768]{2,1,0:T(8,128)(2,1)}, u32[]{:S(2)}, u32[]{:S(2)}) collective-permute-start(bf16[8,96,768]{2,1,0:T(8,128)(2,1)} %bitcast.309), channel_id=1, source_target_pairs={{0,8},{8,0},{16,24},{24,16},{1,9},{9,1},{17,25},{25,17},{2,10},{10... | collective-permute-start | bytes 3538952 | tf_op jit(solution)/shard_map/ppermute | solution.py:132
  258.6 31.1 %all-to-all-start.2 = ((bf16[8,64,768]{2,1,0:T(8,128)(2,1)}), bf16[8,64,768]{2,1,0:T(8,128)(2,1)}, u32[]{:S(2)}, u32[]{:S(2)}) async-start(bf16[8,64,768]{2,1,0:T(8,128)(2,1)} %slice.239), calls=%async_computation.2 | async-start | bytes 1572864 | tf_op jit(solution)/shard_map/all_to_all | solution.py:684
  291.7 37.8 %all-to-all-start.3 = ((bf16[8,64,768]{2,1,0:T(8,128)(2,1)}), bf16[8,64,768]{2,1,0:T(8,128)(2,1)}, u32[]{:S(2)}, u32[]{:S(2)}) async-start(bf16[8,64,768]{2,1,0:T(8,128)(2,1)} %slice.190), calls=%async_computation.3 | async-start | bytes 1572864 | tf_op jit(solution)/shard_map/all_to_all | solution.py:684
  298.4 39.2 %collective-permute-start.47 = (bf16[4,232,768]{2,1,0:T(8,128)(2,1)}, bf16[4,232,768]{2,1,0:T(8,128)(2,1)}, u32[]{:S(2)}, u32[]{:S(2)}) collective-permute-start(bf16[4,232,768]{2,1,0:T(8,128)(2,1)} %dynamic-slice_bitcast_fusion), channel_id=1, source_target_pairs={{0,1},{1,0},{2,3},{3,2},{4,5},{5,4},{6,7},{7,6},{8,9},{9,8},{10,11... | collective-permute-start | bytes 4276232 | tf_op jit(solution)/shard_map/ppermute | solution.py:129
  301.3 28.2 %collective-permute-start.42 = (bf16[1024,384]{1,0:T(8,128)(2,1)}, bf16[1024,384]{1,0:T(8,128)(2,1)}, u32[]{:S(2)}, u32[]{:S(2)}) collective-permute-start(bf16[1024,384]{1,0:T(8,128)(2,1)} %pad_maximum_fusion.2), channel_id=1, source_target_pairs={{0,16},{8,24},{16,0},{24,8},{1,17},{9,25},{17,1},{25,9},{2,18},{10... | collective-permute-start | bytes 2359304 | tf_op jit(solution)/shard_map/ppermute | solution.py:132
  308.5 20.7 %collective-permute-start.44 = (bf16[96,768]{1,0:T(8,128)(2,1)}, bf16[96,768]{1,0:T(8,128)(2,1)}, u32[]{:S(2)}, u32[]{:S(2)}) collective-permute-start(bf16[96,768]{1,0:T(8,128)(2,1)} %get-tuple-element.290), channel_id=1, source_target_pairs={{0,4},{1,5},{2,6},{3,7},{4,0},{5,1},{6,2},{7,3},{8,12},{9,13},{10,... | collective-permute-start | bytes 442376 | tf_op jit(solution)/shard_map/ppermute | solution.py:124
  308.5 20.7 %collective-permute-start.43 = (bf16[96,768]{1,0:T(8,128)(2,1)}, bf16[96,768]{1,0:T(8,128)(2,1)}, u32[]{:S(2)}, u32[]{:S(2)}) collective-permute-start(bf16[96,768]{1,0:T(8,128)(2,1)} %get-tuple-element.291), channel_id=1, source_target_pairs={{0,2},{1,3},{2,4},{3,5},{4,6},{5,7},{6,0},{7,1},{8,10},{9,11},{10,... | collective-permute-start | bytes 442376 | tf_op jit(solution)/shard_map/ppermute | solution.py:124
  313.1 54.1 %collective-permute-start.52 = (s32[2048]{0:T(1024)S(1)}, s32[2048]{0:T(1024)S(1)}, u32[]{:S(2)}, u32[]{:S(2)}) collective-permute-start(s32[2048]{0:T(1024)S(1)} %eq.144), channel_id=1, source_target_pairs={{0,16},{8,24},{16,0},{24,8},{1,17},{9,25},{17,1},{25,9},{2,18},{10... | collective-permute-start | bytes 24584 | tf_op jit(solution)/shard_map/ppermute | solution.py:132
  329.3 22.2 %collective-permute-start.51 = (bf16[96,768]{1,0:T(8,128)(2,1)}, bf16[96,768]{1,0:T(8,128)(2,1)}, u32[]{:S(2)}, u32[]{:S(2)}) collective-permute-start(bf16[96,768]{1,0:T(8,128)(2,1)} %get-tuple-element.286), channel_id=1, source_target_pairs={{0,6},{1,7},{2,0},{3,1},{4,2},{5,3},{6,4},{7,5},{8,14},{9,15},{10,... | collective-permute-start | bytes 442376 | tf_op jit(solution)/shard_map/ppermute | solution.py:124
  329.3 22.2 %collective-permute-start.50 = (bf16[96,768]{1,0:T(8,128)(2,1)}, bf16[96,768]{1,0:T(8,128)(2,1)}, u32[]{:S(2)}, u32[]{:S(2)}) collective-permute-start(bf16[96,768]{1,0:T(8,128)(2,1)} %get-tuple-element.287), channel_id=1, source_target_pairs={{0,4},{1,5},{2,6},{3,7},{4,0},{5,1},{6,2},{7,3},{8,12},{9,13},{10,... | collective-permute-start | bytes 442376 | tf_op jit(solution)/shard_map/ppermute | solution.py:124
  364.9 30.1 %collective-permute-start.55 = (bf16[232,768]{1,0:T(8,128)(2,1)S(1)}, bf16[232,768]{1,0:T(8,128)(2,1)S(1)}, u32[]{:S(2)}, u32[]{:S(2)}) collective-permute-start(bf16[232,768]{1,0:T(8,128)(2,1)S(1)} %get-tuple-element.272), channel_id=1, source_target_pairs={{0,4},{1,5},{2,6},{3,7},{4,0},{5,1},{6,2},{7,3},{8,12},{9,13},{10,... | collective-permute-start | bytes 1069064 | tf_op jit(solution)/shard_map/ppermute | solution.py:124
  365.2 29.8 %collective-permute-start.54 = (bf16[232,768]{1,0:T(8,128)(2,1)S(1)}, bf16[232,768]{1,0:T(8,128)(2,1)S(1)}, u32[]{:S(2)}, u32[]{:S(2)}) collective-permute-start(bf16[232,768]{1,0:T(8,128)(2,1)S(1)} %get-tuple-element.273), channel_id=1, source_target_pairs={{0,2},{1,3},{2,4},{3,5},{4,6},{5,7},{6,0},{7,1},{8,10},{9,11},{10,... | collective-permute-start | bytes 1069064 | tf_op jit(solution)/shard_map/ppermute | solution.py:124
  395.0 36.1 %collective-permute-start.57 = (bf16[3840,384]{1,0:T(8,128)(2,1)S(1)}, bf16[3840,384]{1,0:T(8,128)(2,1)}, u32[]{:S(2)}, u32[]{:S(2)}) collective-permute-start(bf16[3840,384]{1,0:T(8,128)(2,1)S(1)} %add_convert_fusion.here_ref), channel_id=1, source_target_pairs={{0,8},{8,0},{16,24},{24,16},{1,9},{9,1},{17,25},{25,17},{2,10},{10... | collective-permute-start | bytes 8847368 | tf_op jit(solution)/shard_map/ppermute | solution.py:132
  (117 other events, 1163.2 us)
